TPU v7x, 256 devices: a whole 4x4x8 slice. The times are simulated.
256 devices in a mesh: dp: 8 (over z), expert: 32 (over x, y, core).
Axes of the slice: x: 4, y: 4, z: 8, core: 2. Of those that a mesh axis runs over, the one named last changes fastest.
Arguments:
- tokens: bfloat16 [4096, 3584], P('expert', 'dp'), may hold values from -6 to 6
- cotangent: bfloat16 [4096, 3584], P('expert', 'dp'), may hold values from -6 to 6
- slot_ids: int32 [4096, 8], P('expert'), may hold values from 0 to 63, all different within a row; in each aligned block of 128 rows (0 to 127, 128 to 255, ...) at most 20 rows name the same one
- gates: float32 [4096, 8], P('expert'), may hold values from 0.05 to 1
- plan: int32 [32], replicated, may hold values from 0 to 31
- w_gate: bfloat16 [32, 3584, 1024], P('expert', 'dp'), may hold values from -0.09375 to 0.09375
- w_up: bfloat16 [32, 3584, 1024], P('expert', 'dp'), may hold values from -0.09375 to 0.09375
- w_down: bfloat16 [32, 1024, 3584], P('expert', None, 'dp'), may hold values from -0.1875 to 0.1875
Outputs:
- output: bfloat16 [4096, 3584], P('expert', 'dp')
- token_grad: bfloat16 [4096, 3584], P('expert', 'dp')
- grad_gate: float32 [32, 3584, 1024], P('expert', 'dp')
- grad_up: float32 [32, 3584, 1024], P('expert', 'dp')
- grad_down: float32 [32, 1024, 3584], P('expert', None, 'dp')
Inputs may be any that keep to these rules, and one draw needn't show every extreme that they name: `slot_ids`: each row names 8 different slots. Within the 128 rows of one device no slot is named more than 20 times, a bound that some block reaches.
All inputs are finite; a program needn't handle non-finite values.
Results may differ from a plain program's by a relative error of at most 0.029.
Values may be sent and summed in bfloat16 or wider, within the bound.
A program may use at most 128 MiB of HBM per device.

v0:
```python
import jax
import jax.numpy as jnp
from jax import lax
from jax.sharding import PartitionSpec as P


def slope_pair(grad, gate_sum, up_sum):
    sig = jax.nn.sigmoid(gate_sum)
    gate_slope = (grad * up_sum * sig * (1.0 + gate_sum * (1.0 - sig))).astype(jnp.bfloat16)
    up_slope = (grad * jax.nn.silu(gate_sum)).astype(jnp.bfloat16)
    return (gate_slope, up_slope)


def body(tokens, cotangent, slot_ids, gates, plan, w_gate, w_up, w_down):
    expert_count = lax.axis_size("expert")
    token_count, local_width = tokens.shape
    choose_count = slot_ids.shape[1]
    hidden_width = w_gate.shape[2]
    slot_count = 2 * expert_count
    capacity = 5 * token_count * choose_count // (4 * slot_count)
    choice_count = token_count * choose_count
    row_count = expert_count * capacity
    piece_rows = local_width // expert_count
    piece_hidden = hidden_width // expert_count
    home_gate = w_gate[0]
    home_up = w_up[0]
    home_down = w_down[0]
    held_gate, held_up, held_down = (
        lax.all_to_all(
            home_gate.reshape(expert_count, piece_rows, hidden_width),
            "expert",
            split_axis=0,
            concat_axis=0,
            tiled=True,
        ),
        lax.all_to_all(
            home_up.reshape(expert_count, piece_rows, hidden_width),
            "expert",
            split_axis=0,
            concat_axis=0,
            tiled=True,
        ),
        lax.all_to_all(
            home_down.reshape(expert_count, piece_hidden, local_width),
            "expert",
            split_axis=0,
            concat_axis=0,
            tiled=True,
        ),
    )
    pick_gate, pick_up, pick_down = (
        lax.all_to_all(
            jnp.take(held_gate, plan, axis=0), "expert", split_axis=0, concat_axis=0, tiled=True
        ),
        lax.all_to_all(
            jnp.take(held_up, plan, axis=0), "expert", split_axis=0, concat_axis=0, tiled=True
        ),
        lax.all_to_all(
            jnp.take(held_down, plan, axis=0), "expert", split_axis=0, concat_axis=0, tiled=True
        ),
    )
    gate_pair = jnp.stack([home_gate, pick_gate.reshape(local_width, hidden_width)])
    up_pair = jnp.stack([home_up, pick_up.reshape(local_width, hidden_width)])
    down_pair = jnp.stack([home_down, pick_down.reshape(hidden_width, local_width)])
    flat_slots = slot_ids.reshape(-1)
    onehot = (flat_slots[:, None] == jnp.arange(slot_count, dtype=jnp.int32)[None, :]).astype(
        jnp.int32
    )
    position = jnp.sum(jnp.cumsum(onehot, axis=0) * onehot, axis=1) - 1
    place = flat_slots * capacity + position
    inverse = (
        jnp.full((slot_count * capacity,), choice_count, jnp.int32)
        .at[place]
        .set(jnp.arange(choice_count, dtype=jnp.int32))
    )
    token_rows = inverse // choose_count
    tokens_pad = jnp.concatenate([tokens, jnp.zeros((1, local_width), tokens.dtype)])
    cot_pad = jnp.concatenate([cotangent, jnp.zeros((1, local_width), cotangent.dtype)])
    gate_pad = jnp.concatenate([gates.reshape(-1), jnp.zeros((1,), jnp.float32)])
    x_send = tokens_pad[token_rows].reshape(2, expert_count, capacity, local_width)
    z_send = (
        (gate_pad[inverse][:, None] * cot_pad[token_rows].astype(jnp.float32))
        .astype(jnp.bfloat16)
        .reshape(2, expert_count, capacity, local_width)
    )
    x_recv, z_recv = (
        lax.all_to_all(x_send, "expert", split_axis=1, concat_axis=1, tiled=True),
        lax.all_to_all(z_send, "expert", split_axis=1, concat_axis=1, tiled=True),
    )
    x_rows = x_recv.reshape(2, row_count, local_width)
    z_rows = z_recv.reshape(2, row_count, local_width)
    gate_part = jnp.einsum("krd,kdh->krh", x_rows, gate_pair, preferred_element_type=jnp.float32)
    up_part = jnp.einsum("krd,kdh->krh", x_rows, up_pair, preferred_element_type=jnp.float32)
    gate_share, up_share = (
        lax.psum_scatter(
            gate_part.astype(jnp.bfloat16), "dp", scatter_dimension=2, tiled=True
        ).astype(jnp.float32),
        lax.psum_scatter(
            up_part.astype(jnp.bfloat16), "dp", scatter_dimension=2, tiled=True
        ).astype(jnp.float32),
    )
    hidden = lax.all_gather(
        (jax.nn.silu(gate_share) * up_share).astype(jnp.bfloat16), "dp", axis=2, tiled=True
    )
    expert_out = (
        jnp.einsum("krh,khd->krd", hidden, down_pair, preferred_element_type=jnp.float32)
        .astype(jnp.bfloat16)
        .reshape(2, expert_count, capacity, local_width)
    )
    out_back = lax.all_to_all(expert_out, "expert", split_axis=1, concat_axis=1, tiled=True)
    grad_part = jnp.einsum("krd,khd->krh", z_rows, down_pair, preferred_element_type=jnp.float32)
    share_gate, share_up = slope_pair(
        lax.psum_scatter(
            grad_part.astype(jnp.bfloat16), "dp", scatter_dimension=2, tiled=True
        ).astype(jnp.float32),
        gate_share,
        up_share,
    )
    gate_slope, up_slope = (
        lax.all_gather(share_gate, "dp", axis=2, tiled=True),
        lax.all_gather(share_up, "dp", axis=2, tiled=True),
    )
    back_out = (
        (
            jnp.einsum("krh,kdh->krd", gate_slope, gate_pair, preferred_element_type=jnp.float32)
            + jnp.einsum("krh,kdh->krd", up_slope, up_pair, preferred_element_type=jnp.float32)
        )
        .astype(jnp.bfloat16)
        .reshape(2, expert_count, capacity, local_width)
    )
    slope_back = lax.all_to_all(back_out, "expert", split_axis=1, concat_axis=1, tiled=True)
    chosen_out = (
        out_back.reshape(slot_count * capacity, local_width)[place]
        .astype(jnp.float32)
        .reshape(token_count, choose_count, local_width)
    )
    output = jnp.sum(gates[:, :, None] * chosen_out, axis=1).astype(jnp.bfloat16)
    chosen_back = (
        slope_back.reshape(slot_count * capacity, local_width)[place]
        .astype(jnp.float32)
        .reshape(token_count, choose_count, local_width)
    )
    token_grad = jnp.sum(chosen_back, axis=1).astype(jnp.bfloat16)
    grad_gate_pair = jnp.einsum(
        "krd,krh->kdh", x_rows, gate_slope, preferred_element_type=jnp.float32
    )
    grad_up_pair = jnp.einsum("krd,krh->kdh", x_rows, up_slope, preferred_element_type=jnp.float32)
    grad_down_pair = jnp.einsum("krh,krd->khd", hidden, z_rows, preferred_element_type=jnp.float32)
    parts_gate, parts_up, parts_down = (
        lax.all_to_all(
            grad_gate_pair[1].astype(jnp.bfloat16).reshape(expert_count, piece_rows, hidden_width),
            "expert",
            split_axis=0,
            concat_axis=0,
            tiled=True,
        ),
        lax.all_to_all(
            grad_up_pair[1].astype(jnp.bfloat16).reshape(expert_count, piece_rows, hidden_width),
            "expert",
            split_axis=0,
            concat_axis=0,
            tiled=True,
        ),
        lax.all_to_all(
            grad_down_pair[1].astype(jnp.bfloat16).reshape(expert_count, piece_hidden, local_width),
            "expert",
            split_axis=0,
            concat_axis=0,
            tiled=True,
        ),
    )
    member = (plan[None, :] == jnp.arange(expert_count, dtype=jnp.int32)[:, None]).astype(
        jnp.bfloat16
    )
    grouped_gate = jnp.einsum(
        "ej,jrh->erh", member, parts_gate, preferred_element_type=jnp.float32
    ).astype(jnp.bfloat16)
    grouped_up = jnp.einsum(
        "ej,jrh->erh", member, parts_up, preferred_element_type=jnp.float32
    ).astype(jnp.bfloat16)
    grouped_down = jnp.einsum(
        "ej,jhd->ehd", member, parts_down, preferred_element_type=jnp.float32
    ).astype(jnp.bfloat16)
    summed_gate, summed_up, summed_down = (
        lax.all_to_all(grouped_gate, "expert", split_axis=0, concat_axis=0, tiled=True),
        lax.all_to_all(grouped_up, "expert", split_axis=0, concat_axis=0, tiled=True),
        lax.all_to_all(grouped_down, "expert", split_axis=0, concat_axis=0, tiled=True),
    )
    grad_gate = (
        grad_gate_pair[0] + summed_gate.reshape(local_width, hidden_width).astype(jnp.float32)
    )[None]
    grad_up = (grad_up_pair[0] + summed_up.reshape(local_width, hidden_width).astype(jnp.float32))[
        None
    ]
    grad_down = (
        grad_down_pair[0] + summed_down.reshape(hidden_width, local_width).astype(jnp.float32)
    )[None]
    return (output, token_grad, grad_gate, grad_up, grad_down)


def solution(mesh):
    in_specs = (
        P("expert", "dp"),
        P("expert", "dp"),
        P("expert", None),
        P("expert", None),
        P(),
        P("expert", "dp", None),
        P("expert", "dp", None),
        P("expert", None, "dp"),
    )
    out_specs = (
        P("expert", "dp"),
        P("expert", "dp"),
        P("expert", "dp", None),
        P("expert", "dp", None),
        P("expert", None, "dp"),
    )
    return jax.shard_map(body, mesh=mesh, in_specs=in_specs, out_specs=out_specs, check_vma=False)
```

profile of v0, /device:TPU:1, one launch (start us, length us, event | category | flops | bytes accessed | tf_op | source)
XLA Modules:
  0.0 632.1 jit_solution(13110257259999481850)
XLA Ops:
  9.4 8.6 %all-to-all-start.5 = ((bf16[32,32,448]{2,1,0:T(8,128)(2,1)}), bf16[32,32,448]{2,1,0:T(8,128)(2,1)}, u32[]{:S(2)}, u32[]{:S(2)}) async-start(bf16[32,32,448]{2,1,0:T(8,128)(2,1)} %bitcast.5), calls=%async_computation.5 | async-start | bytes 2097152 | tf_op jit(solution)/shard_map/all_to_all | solution.py:43
  18.6 18.0 %reduce-window.6 = s32[64,8,128]{2,1,0:T(8,128)S(1)} reduce-window(s32[64,8,128]{2,1,0:T(8,128)S(1)} %fusion.15, s32[]{:T(128)} %constant.41.clone.1), window={size=1x1x128 pad=0_0x0_0x127_0}, to_apply=%region_0.1 | reduce-window | flops 8323072 | bytes 524292 | tf_op jit(solution)/shard_map/reduce-window
  41.8 4.7 gather_fusion.4
  49.7 7.1 %gather_fusion.3 = f32[1280]{0:T(1024)S(1)} fusion(f32[1025]{0:T(1024)S(1)} %pad_maximum_fusion.3, s32[2048]{0:T(1024)S(1)} %get-tuple-element.18), kind=kCustom, calls=%fused_computation.5 | custom fusion | bytes 15360 | tf_op jit(solution)/shard_map/gather | solution.py:82
  59.6 7.5 %all-to-all-start.8 = ((bf16[2,32,20,448]{3,0,2,1:T(2,128)(2,1)}), bf16[2,32,20,448]{3,0,2,1:T(2,128)(2,1)S(1)}, u32[]{:S(2)}, u32[]{:S(2)}) async-start(bf16[2,32,20,448]{3,0,2,1:T(2,128)(2,1)} %copy.73), calls=%async_computation.8 | async-start | bytes 2621440 | tf_op jit(solution)/shard_map/all_to_all | solution.py:88
  70.2 16.8 %all-to-all-done.8 = bf16[2,32,20,448]{3,0,2,1:T(2,128)(2,1)S(1)} async-done(((bf16[2,32,20,448]{3,0,2,1:T(2,128)(2,1)}), bf16[2,32,20,448]{3,0,2,1:T(2,128)(2,1)S(1)}, u32[]{:S(2)}, u32[]{:S(2)}) %all-to-all-start.8) | async-done | bytes 1146912 | tf_op jit(solution)/shard_map/all_to_all | solution.py:88
  92.1 15.8 %all-to-all-done.6 = bf16[32,32,448]{2,1,0:T(8,128)(2,1)S(1)} async-done(((bf16[32,32,448]{2,1,0:T(8,128)(2,1)}), bf16[32,32,448]{2,1,0:T(8,128)(2,1)S(1)}, u32[]{:S(2)}, u32[]{:S(2)}) %all-to-all-start.6) | async-done | bytes 917536 | tf_op jit(solution)/shard_map/all_to_all | solution.py:58
  113.5 7.0 %copy.94 = bf16[2,640,1024]{1,0,2:T(2,128)(2,1)S(1)} copy(bf16[2,640,1024]{2,1,0:T(8,128)(2,1)} %convolution_convert_fusion) | data formatting | bytes 5242880
  130.0 15.7 %all-to-all-done.1 = bf16[32,14,1024]{2,1,0:T(8,128)(2,1)S(1)} async-done(((bf16[32,14,1024]{2,1,0:T(8,128)(2,1)}), bf16[32,14,1024]{2,1,0:T(8,128)(2,1)S(1)}, u32[]{:S(2)}, u32[]{:S(2)}) %all-to-all-start.1) | async-done | bytes 917536 | tf_op jit(solution)/shard_map/all_to_all | solution.py:29
  145.7 4.7 all-to-all-start.3
  157.5 9.8 %all-to-all-done.3 = bf16[32,14,1024]{2,1,0:T(8,128)(2,1)} async-done(((bf16[32,14,1024]{2,1,0:T(8,128)(2,1)}), bf16[32,14,1024]{2,1,0:T(8,128)(2,1)}, u32[]{:S(2)}, u32[]{:S(2)}) %all-to-all-start.3) | async-done | bytes 917536 | tf_op jit(solution)/shard_map/all_to_all | solution.py:36
  175.3 15.7 %all-to-all-done = bf16[2,32,20,448]{3,0,2,1:T(2,128)(2,1)S(1)} async-done(((bf16[2,32,20,448]{3,0,2,1:T(2,128)(2,1)}), bf16[2,32,20,448]{3,0,2,1:T(2,128)(2,1)S(1)}, u32[]{:S(2)}, u32[]{:S(2)}) %all-to-all-start) | async-done | bytes 1146912 | tf_op jit(solution)/shard_map/all_to_all | solution.py:87
  197.2 14.8 %all-to-all-done.2 = bf16[32,14,1024]{2,1,0:T(8,128)(2,1)S(1)} async-done(((bf16[32,14,1024]{2,1,0:T(8,128)(2,1)}), bf16[32,14,1024]{2,1,0:T(8,128)(2,1)S(1)}, u32[]{:S(2)}, u32[]{:S(2)}) %all-to-all-start.2) | async-done | bytes 917536 | tf_op jit(solution)/shard_map/all_to_all | solution.py:52
  217.8 7.0 %copy.90 = bf16[2,640,1024]{1,0,2:T(2,128)(2,1)S(1)} copy(bf16[2,640,1024]{2,1,0:T(8,128)(2,1)} %convolution_convert_fusion.2) | data formatting | bytes 5242880
  231.9 15.9 %all-to-all-done.4 = bf16[32,14,1024]{2,1,0:T(8,128)(2,1)S(1)} async-done(((bf16[32,14,1024]{2,1,0:T(8,128)(2,1)}), bf16[32,14,1024]{2,1,0:T(8,128)(2,1)S(1)}, u32[]{:S(2)}, u32[]{:S(2)}) %all-to-all-start.4) | async-done | bytes 917536 | tf_op jit(solution)/shard_map/all_to_all | solution.py:55
  249.1 4.7 convolution_convert_fusion.1
  253.7 7.0 %copy.92 = bf16[2,640,1024]{1,0,2:T(2,128)(2,1)S(1)} copy(bf16[2,640,1024]{2,1,0:T(8,128)(2,1)} %convolution_convert_fusion.1) | data formatting | bytes 5242880
  267.9 44.2 %reduce-scatter.12.cloned.1.call-done = bf16[128,1280]{1,0:T(8,128)(2,1)} async-done(((bf16[1024,1280]{1,0:T(8,128)(2,1)}), bf16[128,1280]{1,0:T(8,128)(2,1)}) %reduce-scatter.12.cloned.1.call-update) | async-done | bytes 327696
  316.3 49.9 %all-gather.6.cloned.1.call-done = bf16[2,640,1024]{2,1,0:T(8,128)(2,1)} async-done(((bf16[2,640,128]{2,1,0:T(8,128)(2,1)}), bf16[2,640,1024]{2,1,0:T(8,128)(2,1)}) %all-gather.6.cloned.1.call-update) | async-done | bytes 2621456 | tf_op jit(solution)/shard_map/all_gather | solution.py:120
  372.7 11.3 %all-to-all-start.10 = ((bf16[32,14,1024]{2,1,0:T(8,128)(2,1)}), bf16[32,14,1024]{2,1,0:T(8,128)(2,1)S(1)}, u32[]{:S(2)}, u32[]{:S(2)}) async-start(bf16[32,14,1024]{2,1,0:T(8,128)(2,1)} %convert_element_type.144), calls=%async_computation.10 | async-start | bytes 2097152 | tf_op jit(solution)/shard_map/all_to_all | solution.py:150
  384.0 33.7 %all-gather.8.cloned.1.call-done = bf16[2,640,1024]{2,1,0:T(8,128)(2,1)} async-done(((bf16[2,640,128]{2,1,0:T(8,128)(2,1)}), bf16[2,640,1024]{2,1,0:T(8,128)(2,1)}) %all-gather.8.cloned.1.call-update) | async-done | bytes 2621456 | tf_op jit(solution)/shard_map/all_gather | solution.py:121
  424.2 11.3 %all-to-all-start.12 = ((bf16[32,14,1024]{2,1,0:T(8,128)(2,1)}), bf16[32,14,1024]{2,1,0:T(8,128)(2,1)S(1)}, u32[]{:S(2)}, u32[]{:S(2)}) async-start(bf16[32,14,1024]{2,1,0:T(8,128)(2,1)} %convert_element_type.148), calls=%async_computation.12 | async-start | bytes 2097152 | tf_op jit(solution)/shard_map/all_to_all | solution.py:157
  435.5 33.7 %all-gather.4.cloned.1.call-done = bf16[2,640,1024]{2,1,0:T(8,128)(2,1)} async-done(((bf16[2,640,128]{2,1,0:T(8,128)(2,1)}), bf16[2,640,1024]{2,1,0:T(8,128)(2,1)}) %all-gather.4.cloned.1.call-update) | async-done | bytes 2621456 | tf_op jit(solution)/shard_map/all_gather | solution.py:102
  475.9 11.3 %all-to-all-start.14 = ((bf16[32,32,448]{2,1,0:T(8,128)(2,1)}), bf16[32,32,448]{2,1,0:T(8,128)(2,1)S(1)}, u32[]{:S(2)}, u32[]{:S(2)}) async-start(bf16[32,32,448]{2,1,0:T(8,128)(2,1)} %bitcast.13), calls=%async_computation.14 | async-start | bytes 2097152 | tf_op jit(solution)/shard_map/all_to_all | solution.py:164
  493.8 10.2 %all-to-all-done.14 = bf16[32,32,448]{2,1,0:T(8,128)(2,1)S(1)} async-done(((bf16[32,32,448]{2,1,0:T(8,128)(2,1)}), bf16[32,32,448]{2,1,0:T(8,128)(2,1)S(1)}, u32[]{:S(2)}, u32[]{:S(2)}) %all-to-all-start.14) | async-done | bytes 917536 | tf_op jit(solution)/shard_map/all_to_all | solution.py:164
  517.4 11.7 %all-to-all-done.7 = bf16[2,32,20,448]{3,0,2,1:T(2,128)(2,1)S(1)} async-done(((bf16[2,32,20,448]{3,0,2,1:T(2,128)(2,1)}), bf16[2,32,20,448]{3,0,2,1:T(2,128)(2,1)S(1)}, u32[]{:S(2)}, u32[]{:S(2)}) %all-to-all-start.7) | async-done | bytes 1146912 | tf_op jit(solution)/shard_map/all_to_all | solution.py:110
  537.1 15.9 %all-to-all-done.9 = bf16[2,32,20,448]{3,0,2,1:T(2,128)(2,1)S(1)} async-done(((bf16[2,32,20,448]{3,0,2,1:T(2,128)(2,1)}), bf16[2,32,20,448]{3,0,2,1:T(2,128)(2,1)S(1)}, u32[]{:S(2)}, u32[]{:S(2)}) %all-to-all-start.9) | async-done | bytes 1146912 | tf_op jit(solution)/shard_map/all_to_all | solution.py:131
  561.7 13.0 %all-to-all-done.11 = bf16[32,14,1024]{2,1,0:T(8,128)(2,1)} async-done(((bf16[32,14,1024]{2,1,0:T(8,128)(2,1)}), bf16[32,14,1024]{2,1,0:T(8,128)(2,1)}, u32[]{:S(2)}, u32[]{:S(2)}) %all-to-all-start.11) | async-done | bytes 917536 | tf_op jit(solution)/shard_map/all_to_all | solution.py:185
  574.7 4.9 all-to-all-start.13
  589.4 5.1 gather_fusion.5
  596.5 5.6 all-to-all-start.15
  612.8 6.2 all-to-all-done.15
  (195 shorter events, 168.1 us)
Async XLA Ops:
  9.4 50.2 %all-to-all-start.5 = ((bf16[32,32,448]{2,1,0:T(8,128)(2,1)}), bf16[32,32,448]{2,1,0:T(8,128)(2,1)}, u32[]{:S(2)}, u32[]{:S(2)}) async-start(bf16[32,32,448]{2,1,0:T(8,128)(2,1)} %bitcast.5), calls=%async_computation.5 | async-start | bytes 2097152 | tf_op jit(solution)/shard_map/all_to_all | solution.py:43
  18.1 19.2 %copy-start.28 = (bf16[128,448]{0,1:T(8,128)(2,1)S(1)}, bf16[128,448]{0,1:T(8,128)(2,1)}, u32[]{:S(2)}) copy-start(bf16[128,448]{0,1:T(8,128)(2,1)} %param.11) | copy-start | bytes 344068
  59.6 27.3 %all-to-all-start.8 = ((bf16[2,32,20,448]{3,0,2,1:T(2,128)(2,1)}), bf16[2,32,20,448]{3,0,2,1:T(2,128)(2,1)S(1)}, u32[]{:S(2)}, u32[]{:S(2)}) async-start(bf16[2,32,20,448]{3,0,2,1:T(2,128)(2,1)} %copy.73), calls=%async_computation.8 | async-start | bytes 2621440 | tf_op jit(solution)/shard_map/all_to_all | solution.py:88
  86.9 21.0 %all-to-all-start.6 = ((bf16[32,32,448]{2,1,0:T(8,128)(2,1)}), bf16[32,32,448]{2,1,0:T(8,128)(2,1)S(1)}, u32[]{:S(2)}, u32[]{:S(2)}) async-start(bf16[32,32,448]{2,1,0:T(8,128)(2,1)} %broadcast_select_fusion.2), calls=%async_computation.6 | async-start | bytes 2097152 | tf_op jit(solution)/shard_map/all_to_all | solution.py:58
  90.9 172.1 %reduce-scatter.14.cloned.1.call-start = ((), (), s32[]{:S(2)}) async-start(), calls=%async_computation.24 | async-start | bytes 2949120
  92.1 17.1 %copy-start.9 = (bf16[2,640,448]{1,2,0:T(8,128)(2,1)}, bf16[2,640,448]{1,2,0:T(8,128)(2,1)S(1)}, u32[]{:S(2)}) copy-start(bf16[2,640,448]{1,2,0:T(8,128)(2,1)S(1)} %copy.74) | copy-start | bytes 3440644
  92.1 17.1 %copy-start.23 = (bf16[1,1024,448]{1,2,0:T(8,128)(2,1)S(1)}, bf16[1,1024,448]{1,2,0:T(8,128)(2,1)}, u32[]{:S(2)}) copy-start(bf16[1,1024,448]{1,2,0:T(8,128)(2,1)} %param.17) | copy-start | bytes 2752516
  124.8 20.9 %all-to-all-start.1 = ((bf16[32,14,1024]{2,1,0:T(8,128)(2,1)}), bf16[32,14,1024]{2,1,0:T(8,128)(2,1)S(1)}, u32[]{:S(2)}, u32[]{:S(2)}) async-start(bf16[32,14,1024]{2,1,0:T(8,128)(2,1)} %reshape_squeeze.9), calls=%async_computation.1 | async-start | bytes 2097152 | tf_op jit(solution)/shard_map/all_to_all | solution.py:29
  128.8 21.7 %copy-start.29 = (bf16[128,448]{0,1:T(8,128)(2,1)S(1)}, bf16[128,448]{0,1:T(8,128)(2,1)}, u32[]{:S(2)}) copy-start(bf16[128,448]{0,1:T(8,128)(2,1)} %param.10) | copy-start | bytes 344068
  145.7 21.6 %all-to-all-start.3 = ((bf16[32,14,1024]{2,1,0:T(8,128)(2,1)}), bf16[32,14,1024]{2,1,0:T(8,128)(2,1)}, u32[]{:S(2)}, u32[]{:S(2)}) async-start(bf16[32,14,1024]{2,1,0:T(8,128)(2,1)} %reshape_squeeze.10), calls=%async_computation.3 | async-start | bytes 2097152 | tf_op jit(solution)/shard_map/all_to_all | solution.py:36
  167.3 23.7 %all-to-all-start = ((bf16[2,32,20,448]{3,0,2,1:T(2,128)(2,1)}), bf16[2,32,20,448]{3,0,2,1:T(2,128)(2,1)S(1)}, u32[]{:S(2)}, u32[]{:S(2)}) async-start(bf16[2,32,20,448]{3,0,2,1:T(2,128)(2,1)} %copy.64), calls=%async_computation | async-start | bytes 2621440 | tf_op jit(solution)/shard_map/all_to_all | solution.py:87
  175.3 19.8 %copy-start.19 = (bf16[1,448,1024]{2,1,0:T(8,128)(2,1)S(1)}, bf16[1,448,1024]{2,1,0:T(8,128)(2,1)}, u32[]{:S(2)}) copy-start(bf16[1,448,1024]{2,1,0:T(8,128)(2,1)} %param.15) | copy-start | bytes 2752516
  191.0 21.0 %all-to-all-start.2 = ((bf16[32,14,1024]{2,1,0:T(8,128)(2,1)}), bf16[32,14,1024]{2,1,0:T(8,128)(2,1)S(1)}, u32[]{:S(2)}, u32[]{:S(2)}) async-start(bf16[32,14,1024]{2,1,0:T(8,128)(2,1)} %get-tuple-element.16), calls=%async_computation.2 | async-start | bytes 2097152 | tf_op jit(solution)/shard_map/all_to_all | solution.py:52
  195.0 71.2 %reduce-scatter.10.cloned.1.call-start = ((), (), s32[]{:S(2)}) async-start(), calls=%async_computation.22 | async-start | bytes 2949120
  226.8 21.0 %all-to-all-start.4 = ((bf16[32,14,1024]{2,1,0:T(8,128)(2,1)}), bf16[32,14,1024]{2,1,0:T(8,128)(2,1)S(1)}, u32[]{:S(2)}, u32[]{:S(2)}) async-start(bf16[32,14,1024]{2,1,0:T(8,128)(2,1)} %get-tuple-element.17), calls=%async_computation.4 | async-start | bytes 2097152 | tf_op jit(solution)/shard_map/all_to_all | solution.py:55
  230.9 81.2 %reduce-scatter.12.cloned.1.call-start = ((), (), s32[]{:S(2)}) async-start(), calls=%async_computation.23 | async-start | bytes 2949120
  231.9 17.1 %copy-start.5 = (bf16[2,640,448]{1,2,0:T(8,128)(2,1)S(1)}, bf16[2,640,448]{1,2,0:T(8,128)(2,1)}, u32[]{:S(2)}) copy-start(bf16[2,640,448]{1,2,0:T(8,128)(2,1)} %copy-done.4) | copy-start | bytes 3440644
  262.8 103.5 %all-gather.6.cloned.1.call-start = ((), (), s32[]{:S(2)}) async-start(), calls=%async_computation.20 | async-start | bytes 2949120 | tf_op jit(solution)/shard_map/all_gather | solution.py:120
  313.1 53.1 %copy-start.6 = (bf16[2,640,448]{1,2,0:T(8,128)(2,1)S(1)}, bf16[2,640,448]{1,2,0:T(8,128)(2,1)}, u32[]{:S(2)}) copy-start(bf16[2,640,448]{1,2,0:T(8,128)(2,1)} %copy-done.4) | copy-start | bytes 3440644
  315.2 102.5 %all-gather.8.cloned.1.call-start = ((), (), s32[]{:S(2)}) async-start(), calls=%async_computation.21 | async-start | bytes 2949120 | tf_op jit(solution)/shard_map/all_gather | solution.py:121
  315.8 153.4 %all-gather.4.cloned.1.call-start = ((), (), s32[]{:S(2)}) async-start(), calls=%async_computation.19 | async-start | bytes 2949120 | tf_op jit(solution)/shard_map/all_gather | solution.py:102
  372.7 51.5 %all-to-all-start.10 = ((bf16[32,14,1024]{2,1,0:T(8,128)(2,1)}), bf16[32,14,1024]{2,1,0:T(8,128)(2,1)S(1)}, u32[]{:S(2)}, u32[]{:S(2)}) async-start(bf16[32,14,1024]{2,1,0:T(8,128)(2,1)} %convert_element_type.144), calls=%async_computation.10 | async-start | bytes 2097152 | tf_op jit(solution)/shard_map/all_to_all | solution.py:150
  423.0 46.2 %copy-start.10 = (bf16[2,640,448]{1,2,0:T(8,128)(2,1)S(1)}, bf16[2,640,448]{1,2,0:T(8,128)(2,1)}, u32[]{:S(2)}) copy-start(bf16[2,640,448]{1,2,0:T(8,128)(2,1)} %copy-done.9) | copy-start | bytes 3440644
  424.2 48.3 %copy-start.16 = (bf16[32,14,1024]{2,1,0:T(8,128)(2,1)}, bf16[32,14,1024]{2,1,0:T(8,128)(2,1)S(1)}, u32[]{:S(2)}) copy-start(bf16[32,14,1024]{2,1,0:T(8,128)(2,1)S(1)} %all-to-all-done.10) | copy-start | bytes 2752516
  424.2 51.6 %all-to-all-start.12 = ((bf16[32,14,1024]{2,1,0:T(8,128)(2,1)}), bf16[32,14,1024]{2,1,0:T(8,128)(2,1)S(1)}, u32[]{:S(2)}, u32[]{:S(2)}) async-start(bf16[32,14,1024]{2,1,0:T(8,128)(2,1)} %convert_element_type.148), calls=%async_computation.12 | async-start | bytes 2097152 | tf_op jit(solution)/shard_map/all_to_all | solution.py:157
  475.9 28.2 %all-to-all-start.14 = ((bf16[32,32,448]{2,1,0:T(8,128)(2,1)}), bf16[32,32,448]{2,1,0:T(8,128)(2,1)S(1)}, u32[]{:S(2)}, u32[]{:S(2)}) async-start(bf16[32,32,448]{2,1,0:T(8,128)(2,1)} %bitcast.13), calls=%async_computation.14 | async-start | bytes 2097152 | tf_op jit(solution)/shard_map/all_to_all | solution.py:164
  505.1 24.0 %all-to-all-start.7 = ((bf16[2,32,20,448]{3,0,2,1:T(2,128)(2,1)}), bf16[2,32,20,448]{3,0,2,1:T(2,128)(2,1)S(1)}, u32[]{:S(2)}, u32[]{:S(2)}) async-start(bf16[2,32,20,448]{3,0,2,1:T(2,128)(2,1)} %bitcast.7), calls=%async_computation.7 | async-start | bytes 2621440 | tf_op jit(solution)/shard_map/all_to_all | solution.py:110
  529.1 23.9 %all-to-all-start.9 = ((bf16[2,32,20,448]{3,0,2,1:T(2,128)(2,1)}), bf16[2,32,20,448]{3,0,2,1:T(2,128)(2,1)S(1)}, u32[]{:S(2)}, u32[]{:S(2)}) async-start(bf16[2,32,20,448]{3,0,2,1:T(2,128)(2,1)} %bitcast.73), calls=%async_computation.9 | async-start | bytes 2621440 | tf_op jit(solution)/shard_map/all_to_all | solution.py:131
  553.0 21.7 %all-to-all-start.11 = ((bf16[32,14,1024]{2,1,0:T(8,128)(2,1)}), bf16[32,14,1024]{2,1,0:T(8,128)(2,1)}, u32[]{:S(2)}, u32[]{:S(2)}) async-start(bf16[32,14,1024]{2,1,0:T(8,128)(2,1)} %copy.79), calls=%async_computation.11 | async-start | bytes 2097152 | tf_op jit(solution)/shard_map/all_to_all | solution.py:185
  561.7 17.9 %copy-start.13 = (bf16[32,32,448]{2,1,0:T(8,128)(2,1)S(1)}, bf16[32,32,448]{2,1,0:T(8,128)(2,1)}, u32[]{:S(2)}) copy-start(bf16[32,32,448]{2,1,0:T(8,128)(2,1)} %copy-done.12) | copy-start | bytes 2752516
  574.7 21.8 %all-to-all-start.13 = ((bf16[32,14,1024]{2,1,0:T(8,128)(2,1)}), bf16[32,14,1024]{2,1,0:T(8,128)(2,1)}, u32[]{:S(2)}, u32[]{:S(2)}) async-start(bf16[32,14,1024]{2,1,0:T(8,128)(2,1)} %copy.82), calls=%async_computation.13 | async-start | bytes 2097152 | tf_op jit(solution)/shard_map/all_to_all | solution.py:186
  596.5 22.5 %all-to-all-start.15 = ((bf16[32,32,448]{2,1,0:T(8,128)(2,1)}), bf16[32,32,448]{2,1,0:T(8,128)(2,1)S(1)}, u32[]{:S(2)}, u32[]{:S(2)}) async-start(bf16[32,32,448]{2,1,0:T(8,128)(2,1)} %copy.86), calls=%async_computation.15 | async-start | bytes 2097152 | tf_op jit(solution)/shard_map/all_to_all | solution.py:187
  (23 other events, 135.0 us)
Sparse Core Ops, SparseCore 0:
  122.5 39.2 reduce-scatter.13
  226.9 39.1 reduce-scatter.9
  268.7 43.2 reduce-scatter.11
  315.3 50.8 all-gather.5
  367.8 49.8 all-gather.7
  419.3 49.8 all-gather.3
where the time goes:
time: 643 us; the launch traced here: 632 us
  waiting for transfers between devices  327 us (51%)
  local copies, waits for them, and re-layouts  119 us (19%)
  starting transfers between devices  98.5 us (15%)
  matrix products  38.4 us (6%)
  other arithmetic  33.5 us (5%)
  between operations  15.5 us (2%)
    all_gather x1, waiting for transfers between devices, body(): lax.all_gather(share_gate, 'dp', axis=2, tiled=True)  49.9 us
    unnamed x9, waiting for transfers between devices  46.7 us
    unnamed x87, local copies, waits for them, and re-layouts  46.5 us
    all_gather x1, waiting for transfers between devices, body(): lax.all_gather(share_up, 'dp', axis=2, tiled=True)  33.7 us
    all_gather x1, waiting for transfers between devices, body(): lax.all_gather((jax.nn.silu(gate_share) * up_share).astype(jnp.bfloat16),...  33.7 us
    another operation x3, other arithmetic  18.2 us
    all_to_all x1, waiting for transfers between devices, body(): lax.all_to_all(z_send, 'expert', split_axis=1, concat_axis=1, tiled=True)  16.8 us
    all_to_all x1, waiting for transfers between devices, body(): lax.all_to_all(back_out, 'expert', split_axis=1, concat_axis=1, tiled=True)  15.9 us
  transfers between devices with their start and end apart: 22, of which 18 were waited for; matrix products, arithmetic and copies ran while one was open for 25% of the time, Pallas kernels for 0%

commit v1 on v0

v1 whole, which is shorter than its diff:
```python
import functools

import jax
import jax.numpy as jnp
from jax import lax
from jax.experimental import pallas as pl
from jax.experimental.pallas import tpu as pltpu
from jax.sharding import PartitionSpec as P

MESH = pl.DeviceIdType.MESH
BF = jnp.bfloat16
F32 = jnp.float32
VMEM = pltpu.VMEM
DEPTH = 2
STRIDE = 11


def greet(axis, peers):
    barrier = pltpu.get_barrier_semaphore()
    for peer in peers:
        pl.semaphore_signal(barrier, inc=1, device_id={axis: peer}, device_id_type=MESH)


def greet_all(axis, count, me):
    barrier = pltpu.get_barrier_semaphore()

    def one(i, carry):
        pl.semaphore_signal(
            barrier, inc=1, device_id={axis: lax.rem(me + i, count)}, device_id_type=MESH
        )
        return carry

    lax.fori_loop(1, count, one, 0)


def each(count, first, function):
    def step(i, carry):
        function(i)
        return carry

    lax.fori_loop(first, count, step, 0)


def matmul(a, b, ca, cb):
    return lax.dot_general(a, b, (((ca,), (cb,)), ((), ())), preferred_element_type=F32)


def layer_kernel(
    count, ring, capacity, ints, flts, sent, weights,
    returned, grads,
    got, home_acts, summed, xs_ref, zs_ref, copied, parts, rep_acts, landed, held_even, held_odd, staged, run, slot_grads, rows_acc, made,
    z_send, z_recv, g_send, g_recv, out_send, out_recv, back_send, back_recv, ex_send, ex_recv, local,
):
    me = lax.axis_index("expert")
    z = lax.axis_index("dp")
    right, left = lax.rem(z + 1, ring), lax.rem(z + ring - 1, ring)
    width, rows = xs_ref.shape[1], xs_ref.shape[2]
    half_hidden = parts.shape[2]
    chunk = half_hidden // ring
    half = chunk // 2
    steps = ring // 2
    pair = 2 * capacity
    row_blocks = 8
    lane_blocks = count // row_blocks
    piece_rows, piece = held_even.shape[1], held_even.shape[2]
    sides = (0, 1)

    greet("dp", (right, left))
    greet_all("expert", count, me)
    pl.semaphore_wait(pltpu.get_barrier_semaphore(), count + 1)

    def peer_of(i):
        return lax.rem(me + STRIDE * i, count)

    def to_peer(src, dst, send, recv, peer):
        return pltpu.make_async_remote_copy(
            src_ref=src, dst_ref=dst, send_sem=send, recv_sem=recv,
            device_id={"expert": peer}, device_id_type=MESH,
        )

    def exchange(src, dst, turn):
        def copy(i):
            peer = peer_of(i)
            return to_peer(
                src.at[peer], dst.at[me], ex_send.at[turn, i], ex_recv.at[turn, i], peer
            )

        own = pltpu.make_async_copy(src.at[me], dst.at[me], local.at[2 + turn])
        own.start()
        each(count, 1, lambda i: copy(i).start())

        def finish():
            own.wait()
            each(count, 1, lambda i: copy(i).wait())

        return finish

    def part_of(block):
        row = pl.multiple_of(lax.div(block, lane_blocks) * piece_rows, 16)
        lane = pl.multiple_of(lax.rem(block, lane_blocks) * piece, piece)
        return (pl.ds(row, piece_rows), pl.ds(lane, piece))

    class Move:
        def __init__(self, turn, source, result, summing):
            self.p, self.source, self.result, self.summing = turn % 2, source, result, summing
            self.held = held_odd if self.p else held_even

        def out_copy(self, i):
            peer = peer_of(i)
            return to_peer(
                self.source.at[part_of(peer)], self.held.at[me],
                out_send.at[self.p, i], out_recv.at[self.p, i], peer,
            )

        def back_copy(self, i):
            peer = peer_of(i)
            return to_peer(
                staged.at[self.p, peer], self.result.at[part_of(me)],
                back_send.at[self.p, i], back_recv.at[self.p, i], peer,
            )

        def own_out(self):
            return pltpu.make_async_copy(
                self.source.at[part_of(me)], self.held.at[me], local.at[0]
            )

        def own_back(self):
            return pltpu.make_async_copy(
                staged.at[self.p, me], self.result.at[part_of(me)], local.at[1]
            )

        def begin(self):
            self.own_out().start()
            each(count, 1, lambda i: self.out_copy(i).start())

        def pass_on(self):
            self.own_out().wait()
            each(count, 1, lambda i: self.out_copy(i).wait())
            if self.summing:
                run[0] = self.held[0].astype(F32)

                def add(r):
                    run[r] = run[ints[1, r]] * flts[0, r] + self.held[r].astype(F32)

                each(count, 1, add)

            def fill(i):
                s = peer_of(i)
                if self.summing:
                    staged[self.p, s] = (run[ints[2, s]] * flts[1, s]).astype(BF)
                else:
                    staged[self.p, s] = self.held[ints[0, s]]

            fill(0)
            self.own_back().start()

            def fill_and_send(i):
                fill(i)
                self.back_copy(i).start()

            each(count, 1, fill_and_send)

        def finish(self):
            self.own_back().wait()
            each(count, 1, lambda i: self.back_copy(i).wait())

    def multiply_parts(w, k, p):
        def for_input(m, src):
            def tile(b):
                lane = pl.ds(pl.multiple_of(b * 128, 128), 128)
                parts[p, m, lane] = matmul(
                    w[pl.ds(m * width, width), lane], src[k], 0, 0
                ).astype(BF)

            each(half_hidden // 128, 0, tile)

        for m in range(3):
            for_input(m, zs_ref if m == 2 else xs_ref)

    tile_rows = width // 4

    def multiply_grads(acts, k, dst):
        for m in range(3):
            src = zs_ref if m == 2 else xs_ref

            def tile(b, m=m, src=src):
                row = pl.multiple_of(b * tile_rows, tile_rows)
                dst[pl.ds(m * width + row, tile_rows)] = matmul(
                    src[k, pl.ds(row, tile_rows)], acts[m], 1, 1
                ).astype(BF)

            each(4, 0, tile)

    def home_grads(h):
        lane = pl.ds(h * half_hidden, half_hidden)
        for m in range(3):
            src = zs_ref if m == 2 else xs_ref

            def tile(b, m=m, src=src):
                row = pl.multiple_of(b * tile_rows, tile_rows)
                at = pl.ds(m * width + row, tile_rows)
                grads[at, lane] = matmul(
                    src[0, pl.ds(row, tile_rows)], home_acts[h, m], 1, 1
                ) + summed[h, at].astype(F32)

            each(4, 0, tile)

    def multiply_rows(w, acts, store):
        def tile(b):
            row = pl.multiple_of(b * tile_rows, tile_rows)
            down = pl.ds(2 * width + row, tile_rows)
            store(row, matmul(w[down], acts[2], 1, 0))
            up = pl.ds(width + row, tile_rows)
            store(
                width + row,
                matmul(w[pl.ds(row, tile_rows)], acts[0], 1, 0)
                + matmul(w[up], acts[1], 1, 0),
            )

        each(4, 0, tile)

    def keep_rows(k):
        def store(row, value):
            rows_acc[k, pl.ds(row, tile_rows)] = value

        return store

    def end_rows(k):
        def store(row, value):
            at = pl.ds(row, tile_rows)
            made[k, at] = (rows_acc[k, at] + value).astype(BF)

        return store

    def sort_rows():
        sources = 8
        for n in range(rows // 128):
            first = min(128 * n // capacity, count - sources)
            block = got[pl.ds(first, sources)].reshape(sources * pair, 2 * width)
            shape = (sources * pair, 128)
            r = lax.broadcasted_iota(jnp.int32, shape, 0)
            lane = lax.broadcasted_iota(jnp.int32, shape, 1) + 128 * n
            inside = lax.rem(r, pair)
            goes_to = (lax.div(r, pair) + first) * capacity + lax.rem(inside, capacity)
            for k in range(2):
                hit = (goes_to == lane) & (lax.div(inside, capacity) == k)
                tile = matmul(block, jnp.where(hit, 1.0, 0.0).astype(BF), 0, 0)
                at = pl.ds(128 * n, 128)
                xs_ref[k, :, at] = tile[:width].astype(BF)
                zs_ref[k, :, at] = tile[width:].astype(BF)

    def unsort_rows(k, first):
        sources, window = 4, 256
        blocks = count // sources

        def block(b):
            start = lax.min(lax.div(b * sources * capacity, 128) * 128, rows - window)
            start = pl.multiple_of(start, 128)
            shape = (sources * pair, window)
            r = lax.broadcasted_iota(jnp.int32, shape, 0)
            lane = lax.broadcasted_iota(jnp.int32, shape, 1) + start
            inside = lax.rem(r, pair)
            comes_from = (lax.div(r, pair) + b * sources) * capacity + lax.rem(inside, capacity)
            hit = (comes_from == lane) & (lax.div(inside, capacity) == k)
            tile = matmul(
                jnp.where(hit, 1.0, 0.0).astype(BF), made[k, :, pl.ds(start, window)], 1, 1
            ).reshape(sources, pair, 2 * width)
            at = pl.ds(b * sources, sources)
            if first:
                got[at] = tile.astype(BF)
            else:
                got[at] = (got[at].astype(F32) + tile).astype(BF)

        each(blocks, 0, block)

    def over_dp(p, acts, early, middle, late):
        def rows_of(c, d=None):
            base = lax.rem(c + 2 * ring, ring) * chunk
            if d is None:
                return pl.ds(pl.multiple_of(base, chunk), chunk)
            return pl.ds(pl.multiple_of(base + d * half, half), half)

        def sum_copy(t, m, d):
            c = z + steps - t if d == 0 else z - steps + t
            if t == 0:
                src = parts.at[p, m, rows_of(c, d)]
                dst = landed.at[p, d, 0, m, pl.ds(d * half, half)]
            else:
                src, dst = landed.at[p, d, t - 1, m], landed.at[p, d, t, m]
            return pltpu.make_async_remote_copy(
                src_ref=src,
                dst_ref=dst,
                send_sem=z_send.at[p, d, t, m],
                recv_sem=z_recv.at[p, d, t, m],
                device_id={"dp": right if d == 0 else left},
                device_id_type=MESH,
            )

        def sum_add(t, m, d):
            c = z + steps - t if d == 0 else z - steps + t
            if t == 1:
                mine, other = pl.ds(d * half, half), pl.ds((1 - d) * half, half)
                landed[p, d, 0, m, mine] = (
                    landed[p, d, 0, m, mine].astype(F32) + parts[p, m, rows_of(c, d)].astype(F32)
                ).astype(BF)
                landed[p, d, 0, m, other] = parts[p, m, rows_of(c, 1 - d)]
            else:
                landed[p, d, t - 1, m] = (
                    landed[p, d, t - 1, m].astype(F32) + parts[p, m, rows_of(c)].astype(F32)
                ).astype(BF)

        def spread_copy(t, m, d):
            c = z - t if d == 0 else z + t
            at = rows_of(c, d) if t == steps - 1 else rows_of(c)
            return pltpu.make_async_remote_copy(
                src_ref=acts.at[m, at],
                dst_ref=acts.at[m, at],
                send_sem=g_send.at[p, d, t, m],
                recv_sem=g_recv.at[p, d, t, m],
                device_id={"dp": right if d == 0 else left},
                device_id_type=MESH,
            )

        in_flight = ([], [])

        def launch(copy, d):
            if len(in_flight[d]) == DEPTH:
                in_flight[d].pop(0).wait_send()
            copy.start()
            in_flight[d].append(copy)

        for m in range(3):
            for d in sides:
                launch(sum_copy(0, m, d), d)
        early()
        for t in range(1, steps):
            for m in range(3):
                for d in sides:
                    sum_copy(t - 1, m, d).wait_recv()
                    sum_add(t, m, d)
                    launch(sum_copy(t, m, d), d)

        def total(m):
            for d in sides:
                sum_copy(steps - 1, m, d).wait_recv()
            return (
                landed[p, 0, steps - 1, m].astype(F32)
                + landed[p, 1, steps - 1, m].astype(F32)
                + parts[p, m, rows_of(z)].astype(F32)
            )

        def spread_first(m, value):
            acts[m, rows_of(z)] = value.astype(BF)
            for d in sides:
                launch(spread_copy(0, m, d), d)

        gate = total(0)
        up = total(1)
        q = jax.nn.sigmoid(gate)
        silu = gate * q
        spread_first(2, silu * up)
        grad = total(2)
        spread_first(0, grad * up * q * (1.0 + gate * (1.0 - q)))
        spread_first(1, grad * silu)
        middle()
        for t in range(1, steps):
            for m in (2, 0, 1):
                for d in sides:
                    spread_copy(t - 1, m, d).wait_recv()
                    launch(spread_copy(t, m, d), d)
            if t == 1:
                late()
        for m in (2, 0, 1):
            for d in sides:
                spread_copy(steps - 1, m, d).wait_recv()
        for d in sides:
            for copy in in_flight[d]:
                copy.wait_send()

    def nothing():
        pass

    moves = [
        Move(0, weights.at[0], copied.at[0], False),
        Move(1, weights.at[1], copied.at[1], False),
        Move(2, slot_grads.at[0], summed.at[0], True),
        Move(3, slot_grads.at[1], summed.at[1], True),
    ]
    pad = slot_grads.shape[1] - 3 * width
    if pad:
        for h in range(2):
            slot_grads[h, pl.ds(3 * width, pad)] = jnp.zeros((pad, half_hidden), BF)
    exchange(sent, got, 0)()
    moves[0].begin()
    sort_rows()
    multiply_parts(weights.at[0], 0, 0)
    over_dp(0, home_acts.at[0], nothing, moves[0].pass_on, nothing)
    moves[0].finish()
    moves[1].begin()
    multiply_parts(copied.at[0], 1, 1)
    over_dp(
        1,
        rep_acts.at[0],
        lambda: multiply_rows(weights.at[0], home_acts.at[0], keep_rows(0)),
        moves[1].pass_on,
        nothing,
    )
    moves[1].finish()
    multiply_parts(copied.at[1], 1, 0)

    def first_grads():
        multiply_grads(rep_acts.at[0], 1, slot_grads.at[0])
        moves[2].begin()
        multiply_rows(copied.at[0], rep_acts.at[0], keep_rows(1))

    over_dp(0, rep_acts.at[1], first_grads, moves[2].pass_on, nothing)
    multiply_parts(weights.at[1], 0, 1)
    moves[2].finish()

    def second_grads():
        multiply_grads(rep_acts.at[1], 1, slot_grads.at[1])
        moves[3].begin()

    def replica_rows():
        multiply_rows(copied.at[1], rep_acts.at[1], end_rows(1))
        unsort_rows(1, True)

    over_dp(1, home_acts.at[1], second_grads, moves[3].pass_on, replica_rows)
    multiply_rows(weights.at[1], home_acts.at[1], end_rows(0))
    unsort_rows(0, False)
    done = exchange(got, returned, 1)
    home_grads(0)
    moves[3].finish()
    home_grads(1)
    done()


def layer(sent, weights, ints, flts, capacity, ring):
    count, pair, two_width = sent.shape
    width = two_width // 2
    flat, half_hidden = weights.shape[1:]
    rows = count * capacity
    steps = ring // 2
    chunk = half_hidden // ring
    piece = (flat // 8, half_hidden * 8 // count)
    sem = pltpu.SemaphoreType.DMA
    acts = (2, 3, half_hidden, rows)
    return pl.pallas_call(
        functools.partial(layer_kernel, count, ring, capacity),
        out_shape=(
            jax.ShapeDtypeStruct(sent.shape, BF),
            jax.ShapeDtypeStruct((3 * width, 2 * half_hidden), F32),
        ),
        in_specs=[pl.BlockSpec(memory_space=pltpu.SMEM)] * 2
        + [pl.BlockSpec(memory_space=VMEM)] * 2,
        out_specs=[pl.BlockSpec(memory_space=VMEM)] * 2,
        scratch_shapes=[
            VMEM(sent.shape, BF),
            VMEM(acts, BF),
            VMEM(weights.shape, BF),
            VMEM((2, width, rows), BF),
            VMEM((2, width, rows), BF),
            VMEM(weights.shape, BF),
            VMEM((2, 3, half_hidden, rows), BF),
            VMEM(acts, BF),
            VMEM((2, 2, steps, 3, chunk, rows), BF),
            VMEM((count,) + piece, BF),
            VMEM((count,) + piece, BF),
            VMEM((2, count) + piece, BF),
            VMEM((count,) + piece, F32),
            VMEM(weights.shape, BF),
            VMEM((2, two_width, rows), F32),
            VMEM((2, two_width, rows), BF),
            sem((2, 2, steps, 3)),
            sem((2, 2, steps, 3)),
            sem((2, 2, steps, 3)),
            sem((2, 2, steps, 3)),
            sem((2, count)),
            sem((2, count)),
            sem((2, count)),
            sem((2, count)),
            sem((2, count)),
            sem((2, count)),
            sem((4,)),
        ],
        compiler_params=pltpu.CompilerParams(
            collective_id=1, has_side_effects=True, vmem_limit_bytes=62 << 20
        ),
        name="layer",
    )(ints, flts, sent, weights)


def body(tokens, cotangent, slot_ids, gates, plan, w_gate, w_up, w_down):
    count = lax.axis_size("expert")
    ring = lax.axis_size("dp")
    token_count, width = tokens.shape
    choose = slot_ids.shape[1]
    hidden = w_gate.shape[2]
    slots = 2 * count
    capacity = 5 * token_count * choose // (4 * slots)
    pair = 2 * capacity
    columns = count * pair
    rows = count * capacity
    half = hidden // 2

    named = slot_ids[:, :, None] == jnp.arange(slots, dtype=jnp.int32)
    names = jnp.sum(named.astype(F32), axis=1)
    t_ids = jnp.arange(token_count, dtype=jnp.int32)
    before = (t_ids[:, None] > t_ids[None, :]).astype(BF)
    turns = jnp.dot(before, names.astype(BF), preferred_element_type=F32)
    turn = jnp.sum(jnp.where(named, turns[:, None, :], 0.0), axis=2).astype(jnp.int32)
    place = (slot_ids % count) * pair + (slot_ids // count) * capacity + turn
    column_ids = jnp.arange(columns, dtype=jnp.int32)
    hits = place[:, :, None] == column_ids
    chosen = jnp.sum(hits.astype(F32), axis=1).astype(BF)
    weight = jnp.sum(jnp.where(hits, gates[:, :, None], 0.0), axis=1)
    gate_of = jnp.sum(weight, axis=0)

    both = jnp.concatenate([tokens, cotangent], axis=1)
    picked = lax.dot_general(chosen, both, (((0,), (0,)), ((), ())), preferred_element_type=F32)
    scale = jnp.where(jnp.arange(2 * width)[None, :] < width, 1.0, gate_of[:, None])
    sent = (picked * scale).astype(BF).reshape(count, pair, 2 * width)
    down_t = jnp.swapaxes(w_down[0], 0, 1)
    flat = -(-3 * width // (8 * 16)) * 8 * 16
    filler = jnp.zeros((flat - 3 * width, hidden), BF)
    whole = jnp.concatenate([w_gate[0], w_up[0], down_t, filler])
    weights = jnp.stack([whole[:, h * half : (h + 1) * half] for h in range(2)])

    s_ids = jnp.arange(count, dtype=jnp.int32)
    sought = jnp.concatenate([plan, s_ids])
    limit = jnp.concatenate([s_ids, jnp.full((count,), count, jnp.int32)])
    match = (plan[None, :] == sought[:, None]) & (s_ids[None, :] < limit[:, None])
    found = jnp.max(jnp.where(match, s_ids[None, :], -1), axis=1)
    ints = jnp.concatenate([plan, jnp.maximum(found, 0)]).reshape(3, count)
    flts = (found >= 0).astype(F32).reshape(2, count)

    returned, grads = layer(sent, weights, ints, flts, capacity, ring)
    returned = returned.reshape(columns, 2 * width)
    high = weight.astype(BF)
    low = (weight - high.astype(F32)).astype(BF)
    output = (
        jnp.dot(high, returned[:, :width], preferred_element_type=F32)
        + jnp.dot(low, returned[:, :width], preferred_element_type=F32)
    ).astype(BF)
    token_grad = jnp.dot(chosen, returned[:, width:], preferred_element_type=F32).astype(BF)

    return (
        output,
        token_grad,
        grads[:width][None],
        grads[width : 2 * width][None],
        jnp.swapaxes(grads[2 * width :], 0, 1)[None],
    )


def solution(mesh):
    in_specs = (
        P("expert", "dp"),
        P("expert", "dp"),
        P("expert", None),
        P("expert", None),
        P(),
        P("expert", "dp", None),
        P("expert", "dp", None),
        P("expert", None, "dp"),
    )
    out_specs = (
        P("expert", "dp"),
        P("expert", "dp"),
        P("expert", "dp", None),
        P("expert", "dp", None),
        P("expert", None, "dp"),
    )
    return jax.shard_map(body, mesh=mesh, in_specs=in_specs, out_specs=out_specs, check_vma=False)
```

time: 643 us -> 300 us (0.47); the launches traced: 632 us -> 300 us
  waiting for transfers between devices: 327 us -> 0 us
  Pallas kernels: 0 us -> 267 us
  local copies, waits for them, and re-layouts: 119 us -> 5.17 us
  starting transfers between devices: 98.5 us -> 0 us
  matrix products: 38.4 us -> 11.3 us
  other arithmetic: 33.5 us -> 16 us
  between operations: 15.5 us -> 0.72 us
    pallas_call x0 -> x1, Pallas kernels: none -> 267 us  [layer(): pl.pallas_call(functools.partial(layer_kernel, count, ring, capacity), ou...]
    all_to_all x16 -> x0, waiting for transfers between devices: 163 us -> none  [the longest x1 16.8 us: body(): lax.all_to_all(z_send, 'expert', split_axis=1, concat_axis=1, tiled=True)]
    all_gather x3 -> x0, waiting for transfers between devices: 117 us -> none  [the longest x1 49.9 us: body(): lax.all_gather(share_gate, 'dp', axis=2, tiled=True)]
    all_to_all x16 -> x0, starting transfers between devices: 98 us -> none  [the longest x1 11.3 us: body(): lax.all_to_all(grad_down_pair[1].astype(jnp.bfloat16).reshape(expert_coun...]
    unnamed x9 -> x0, waiting for transfers between devices: 46.7 us -> none
    unnamed x87 -> x7, local copies, waits for them, and re-layouts: 46.5 us -> 0.8 us
    gather x8 -> x0, local copies, waits for them, and re-layouts: 29.2 us -> none  [the longest x1 7.08 us: body(): gate_pad[inverse][:, None] * cot_pad[token_rows].astype(jnp.float32)]
    dot_general x12 -> x5, matrix products: 38.4 us -> 11.3 us  [the longest x1 3.42 us: body(): jnp.dot(chosen, returned[:, width:], preferred_element_type=F32).astype(BF)]
  transfers between devices with their start and end apart: 22 -> 0, of which waited for: 18 -> 0; matrix products, arithmetic and copies ran while one was open for 25% -> 0% of each run, Pallas kernels for 0% -> 0%
where the time goes in v1:
time: 300 us
  Pallas kernels  267 us (89%)
  other arithmetic  16 us (5%)
  matrix products  11.3 us (4%)
  local copies, waits for them, and re-layouts  5.17 us (2%)
    pallas_call x1, Pallas kernels, layer(): pl.pallas_call(functools.partial(layer_kernel, count, ring, capacity), ou...  267 us
    concatenate x1, other arithmetic, body(): whole = jnp.concatenate([w_gate[0], w_up[0], down_t, filler])  6.11 us

profile of v1, /device:TPU:1, one launch (start us, length us, event | category | flops | bytes accessed | tf_op | source)
XLA Modules:
  0.0 300.1 jit_solution(5915948068177059392)
XLA Ops:
  0.6 0.7 pad_add_fusion
  1.4 0.8 select_reduce_fusion.3
  2.2 0.7 pad_add_fusion.1
  2.9 0.6 reshape.41.flts
  3.5 0.7 reshape.38.ints
  4.2 0.1 pad.6.clone
  4.3 0.7 convert_reduce_fusion.1
  5.0 0.0 copy-start.1
  5.0 0.0 copy-start.2
  5.0 0.1 fusion.18
  5.2 0.8 select_reduce_fusion.2
  6.0 0.7 fusion.23
  6.7 0.1 copy.17
  6.8 0.8 copy.18
  7.6 3.5 %select_reduce_fusion.1 = (f32[128,1280]{1,0:T(8,128)S(1)}, f32[1280]{0:T(1024)S(1)}, bf16[128,1280]{1,0:T(8,128)(2,1)S(1)}) fusion(f32[128,8]{1,0:T(8,128)S(1)} %copy.18, s32[128,8]{1,0:T(8,128)S(1)} %copy.17), kind=kLoop, calls=%fused_computation.1 | loop fusion | flops 7535360 | bytes 996352 | tf_op jit(solution)/shard_map/reduce_sum | solution.py:516
  11.1 3.3 %multiply_convert_fusion = bf16[1280,896]{1,0:T(8,128)(2,1)} fusion(f32[1280]{0:T(1024)S(1)} %get-tuple-element.10, pred[896]{0:T(1024)(128)(4,1)S(1)} %iota_compare_fusion.5, bf16[128,448]{0,1:T(8,128)(2,1)} %param.9, bf16[128,448]{0,1:T(8,128)(2,1)} %param.8, bf16[128,1280]{1,0:T(8,128)(2,1)S(1)} %get-tuple-element.11), kind=kOutput, calls=%fused_computation.4 | convolution fusion | flops 297500672 | bytes 2856832 | tf_op jit(solution)/shard_map/dot_general | solution.py:520
  14.4 0.0 copy-done.1
  14.4 0.0 copy-done.2
  14.4 6.1 %maximum_maximum_fusion = bf16[1408,1024]{1,0:T(8,128)(2,1)S(1)} fusion(bf16[448,1024]{1,0:T(8,128)(2,1)S(1)} %bitcast.26, bf16[448,1024]{1,0:T(8,128)(2,1)S(1)} %bitcast.27, bf16[448,1024]{1,0:T(8,128)(2,1)} %bitcast.28, bf16[1408]{0:T(1024)(128)(2,1)S(1)} %pad.6.clone), kind=kLoop, calls=%fused_computation.5 | loop fusion | flops 11534336 | bytes 5638912 | tf_op jit(solution)/shard_map/concatenate | solution.py:526
  20.5 0.2 slice_bitcast_fusion.4
  20.7 1.8 pad_maximum_fusion.weights
  22.6 267.0 %layer.1 = (bf16[32,40,896]{2,1,0:T(8,128)(2,1)}, f32[1344,1024]{1,0:T(8,128)}) custom-call(s32[3,32]{1,0:T(4,128)} %reshape.38.ints, f32[2,32]{1,0:T(2,128)} %reshape.41.flts, bf16[32,40,896]{2,1,0:T(8,128)(2,1)} %bitcast.25, bf16[2,1408,512]{2,1,0:T(8,128)(2,1)} %pad_maximum_fusion.weights), custom_call_target="tpu_custom_call" | custom-call | tf_op jit(solution)/shard_map/layer/pallas_call | solution.py:448
  289.5 0.0 copy-start
  289.6 3.4 %fusion.8 = bf16[128,448]{0,1:T(8,128)(2,1)} fusion(bf16[1280,896]{1,0:T(8,128)(2,1)} %bitcast.22, bf16[128,1280]{1,0:T(8,128)(2,1)S(1)} %get-tuple-element.11), kind=kOutput, calls=%fused_computation.19 | convolution fusion | flops 146857984 | bytes 1753088 | tf_op jit(solution)/shard_map/dot_general | solution.py:545
  293.0 1.9 fusion.3
  294.9 2.5 fusion.5
  297.4 0.0 copy-done
  297.4 2.7 slice_bitcast_fusion
  (5 shorter events, 0.0 us)
Async XLA Ops:
  5.0 9.4 %copy-start.1 = (bf16[1,1024,448]{1,2,0:T(8,128)(2,1)S(1)}, bf16[1,1024,448]{1,2,0:T(8,128)(2,1)}, u32[]{:S(2)}) copy-start(bf16[1,1024,448]{1,2,0:T(8,128)(2,1)} %param.15) | copy-start | bytes 2752516
  5.0 9.4 %copy-start.2 = (bf16[1,448,1024]{2,1,0:T(8,128)(2,1)S(1)}, bf16[1,448,1024]{2,1,0:T(8,128)(2,1)}, u32[]{:S(2)}) copy-start(bf16[1,448,1024]{2,1,0:T(8,128)(2,1)} %param.14) | copy-start | bytes 2752516
  289.5 7.9 %copy-start = (f32[1344,1024]{1,0:T(8,128)S(1)}, f32[1344,1024]{1,0:T(8,128)}, u32[]{:S(2)}) copy-start(f32[1344,1024]{1,0:T(8,128)} %get-tuple-element.8) | copy-start | bytes 16515076

commit v2 on v1

--- a/solution.py
+++ b/solution.py
@@ -46,10 +46,10 @@
 
 
 def layer_kernel(
-    count, ring, capacity, ints, flts, sent, weights,
-    returned, grads,
-    got, home_acts, summed, xs_ref, zs_ref, copied, parts, rep_acts, landed, held_even, held_odd, staged, run, slot_grads, rows_acc, made,
-    z_send, z_recv, g_send, g_recv, out_send, out_recv, back_send, back_recv, ex_send, ex_recv, local,
+    count, ring, capacity, plan, before_it, last_of, ids, gates, both, w_gate, w_up, w_down,
+    results, grads,
+    weights, sent, returned, chosen, high, low, got, home_acts, summed, xs_ref, zs_ref, copied, parts, rep_acts, landed, held_even, held_odd, staged, run, slot_grads, rows_acc, made,
+    z_send, z_recv, g_send, g_recv, out_send, out_recv, back_send, back_recv, ex_send, ex_recv, local, placed,
 ):
     me = lax.axis_index("expert")
     z = lax.axis_index("dp")
@@ -65,8 +65,24 @@
     piece_rows, piece = held_even.shape[1], held_even.shape[2]
     sides = (0, 1)
 
+    def place_copy(h, m):
+        lane = pl.ds(h * half_hidden, half_hidden)
+        return pltpu.make_async_copy(
+            (w_gate, w_up, w_down)[m].at[:, lane],
+            weights.at[h, pl.ds(m * width, width)],
+            placed.at[h, m],
+        )
+
+    for h in range(2):
+        for m in range(3):
+            place_copy(h, m).start()
     greet("dp", (right, left))
     greet_all("expert", count, me)
+    pad = weights.shape[1] - 3 * width
+    if pad:
+        for h in range(2):
+            for ref in (weights, slot_grads):
+                ref[h, pl.ds(3 * width, pad)] = jnp.zeros((pad, half_hidden), BF)
     pl.semaphore_wait(pltpu.get_barrier_semaphore(), count + 1)
 
     def peer_of(i):
@@ -140,16 +156,20 @@
                 run[0] = self.held[0].astype(F32)
 
                 def add(r):
-                    run[r] = run[ints[1, r]] * flts[0, r] + self.held[r].astype(F32)
+                    prior = before_it[r]
+                    keep = jnp.where(prior >= 0, 1.0, 0.0)
+                    run[r] = run[jnp.maximum(prior, 0)] * keep + self.held[r].astype(F32)
 
                 each(count, 1, add)
 
             def fill(i):
                 s = peer_of(i)
                 if self.summing:
-                    staged[self.p, s] = (run[ints[2, s]] * flts[1, s]).astype(BF)
+                    final = last_of[s]
+                    some = jnp.where(final >= 0, 1.0, 0.0)
+                    staged[self.p, s] = (run[jnp.maximum(final, 0)] * some).astype(BF)
                 else:
-                    staged[self.p, s] = self.held[ints[0, s]]
+                    staged[self.p, s] = self.held[plan[s]]
 
             fill(0)
             self.own_back().start()
@@ -231,6 +251,65 @@
             made[k, at] = (rows_acc[k, at] + value).astype(BF)
 
         return store
+
+    row_tiles = 2
+    tile_columns = count * pair // row_tiles
+    tile_sources = count // row_tiles
+
+    def send_rows():
+        tokens, choose = ids.shape
+        slot = lax.broadcasted_iota(jnp.int32, (tokens, 2 * count), 1)
+        named = [ids[:, k : k + 1] == slot for k in range(choose)]
+        names = sum(jnp.where(hit, 1.0, 0.0) for hit in named)
+        square = (tokens, tokens)
+        earlier = lax.broadcasted_iota(jnp.int32, square, 0) > lax.broadcasted_iota(
+            jnp.int32, square, 1
+        )
+        turns = matmul(jnp.where(earlier, 1.0, 0.0).astype(BF), names.astype(BF), 1, 0)
+        places = []
+        for k in range(choose):
+            turn = jnp.sum(jnp.where(named[k], turns, 0.0), axis=1, keepdims=True)
+            own = ids[:, k : k + 1]
+            kind = jnp.where(own >= count, 1, 0)
+            places.append(
+                (own - kind * count) * pair + kind * capacity + turn.astype(jnp.int32)
+            )
+        for n in range(row_tiles):
+            shape = (tokens, tile_columns)
+            column = lax.broadcasted_iota(jnp.int32, shape, 1) + n * tile_columns
+            picks = jnp.zeros(shape, F32)
+            weight = jnp.zeros(shape, F32)
+            for k in range(choose):
+                hit = places[k] == column
+                picks = picks + jnp.where(hit, 1.0, 0.0)
+                weight = weight + jnp.where(hit, gates[:, k : k + 1], 0.0)
+            at = pl.ds(n * tile_columns, tile_columns)
+            chosen[:, at] = picks.astype(BF)
+            top = weight.astype(BF)
+            high[:, at] = top
+            low[:, at] = (weight - top.astype(F32)).astype(BF)
+            plain = matmul(chosen[:, at], both[...], 0, 0)
+            scaled = matmul(high[:, at], both[...], 0, 0) + matmul(low[:, at], both[...], 0, 0)
+            lane = lax.broadcasted_iota(jnp.int32, plain.shape, 1)
+            sent[pl.ds(n * tile_sources, tile_sources)] = (
+                jnp.where(lane < width, plain, scaled)
+                .astype(BF)
+                .reshape(tile_sources, pair, 2 * width)
+            )
+
+    def add_rows():
+        plain, scaled = 0.0, 0.0
+        for n in range(row_tiles):
+            at = pl.ds(n * tile_columns, tile_columns)
+            block = returned[pl.ds(n * tile_sources, tile_sources)].reshape(
+                tile_columns, 2 * width
+            )
+            plain = plain + matmul(chosen[:, at], block, 1, 0)
+            scaled = scaled + (
+                matmul(high[:, at], block, 1, 0) + matmul(low[:, at], block, 1, 0)
+            )
+        lane = lax.broadcasted_iota(jnp.int32, plain.shape, 1)
+        results[...] = jnp.where(lane < width, scaled, plain).astype(BF)
 
     def sort_rows():
         sources = 8
@@ -386,25 +465,29 @@
         Move(2, slot_grads.at[0], summed.at[0], True),
         Move(3, slot_grads.at[1], summed.at[1], True),
     ]
-    pad = slot_grads.shape[1] - 3 * width
-    if pad:
-        for h in range(2):
-            slot_grads[h, pl.ds(3 * width, pad)] = jnp.zeros((pad, half_hidden), BF)
+    for m in range(3):
+        place_copy(0, m).wait()
+    moves[0].begin()
+    send_rows()
     exchange(sent, got, 0)()
-    moves[0].begin()
+    moves[0].pass_on()
     sort_rows()
     multiply_parts(weights.at[0], 0, 0)
-    over_dp(0, home_acts.at[0], nothing, moves[0].pass_on, nothing)
-    moves[0].finish()
-    moves[1].begin()
+    for m in range(3):
+        place_copy(1, m).wait()
+
+    def next_weights():
+        moves[0].finish()
+        moves[1].begin()
+
+    over_dp(0, home_acts.at[0], nothing, next_weights, nothing)
     multiply_parts(copied.at[0], 1, 1)
-    over_dp(
-        1,
-        rep_acts.at[0],
-        lambda: multiply_rows(weights.at[0], home_acts.at[0], keep_rows(0)),
-        moves[1].pass_on,
-        nothing,
-    )
+
+    def home_rows():
+        moves[1].pass_on()
+        multiply_rows(weights.at[0], home_acts.at[0], keep_rows(0))
+
+    over_dp(1, rep_acts.at[0], home_rows, nothing, nothing)
     moves[1].finish()
     multiply_parts(copied.at[1], 1, 0)
 
@@ -433,34 +516,48 @@
     moves[3].finish()
     home_grads(1)
     done()
-
-
-def layer(sent, weights, ints, flts, capacity, ring):
-    count, pair, two_width = sent.shape
-    width = two_width // 2
-    flat, half_hidden = weights.shape[1:]
+    add_rows()
+
+
+def layer(plan, before_it, last_of, ids, gates, both, w_gate, w_up, w_down, capacity, ring):
+    count = plan.shape[0]
+    tokens, two_width = both.shape
+    width, hidden = w_gate.shape
+    half_hidden = hidden // 2
+    pair = 2 * capacity
     rows = count * capacity
+    columns = count * pair
+    flat = -(-3 * width // (8 * 16)) * 8 * 16
     steps = ring // 2
     chunk = half_hidden // ring
     piece = (flat // 8, half_hidden * 8 // count)
     sem = pltpu.SemaphoreType.DMA
     acts = (2, 3, half_hidden, rows)
+    halves = (2, flat, half_hidden)
+    blocks = (count, pair, two_width)
     return pl.pallas_call(
         functools.partial(layer_kernel, count, ring, capacity),
         out_shape=(
-            jax.ShapeDtypeStruct(sent.shape, BF),
-            jax.ShapeDtypeStruct((3 * width, 2 * half_hidden), F32),
+            jax.ShapeDtypeStruct((tokens, two_width), BF),
+            jax.ShapeDtypeStruct((3 * width, hidden), F32),
         ),
-        in_specs=[pl.BlockSpec(memory_space=pltpu.SMEM)] * 2
-        + [pl.BlockSpec(memory_space=VMEM)] * 2,
+        in_specs=[pl.BlockSpec(memory_space=pltpu.SMEM)] * 3
+        + [pl.BlockSpec(memory_space=VMEM)] * 3
+        + [pl.BlockSpec(memory_space=pl.ANY)] * 3,
         out_specs=[pl.BlockSpec(memory_space=VMEM)] * 2,
         scratch_shapes=[
-            VMEM(sent.shape, BF),
+            VMEM(halves, BF),
+            VMEM(blocks, BF),
+            VMEM(blocks, BF),
+            VMEM((tokens, columns), BF),
+            VMEM((tokens, columns), BF),
+            VMEM((tokens, columns), BF),
+            VMEM(blocks, BF),
             VMEM(acts, BF),
-            VMEM(weights.shape, BF),
+            VMEM(halves, BF),
             VMEM((2, width, rows), BF),
             VMEM((2, width, rows), BF),
-            VMEM(weights.shape, BF),
+            VMEM(halves, BF),
             VMEM((2, 3, half_hidden, rows), BF),
             VMEM(acts, BF),
             VMEM((2, 2, steps, 3, chunk, rows), BF),
@@ -468,7 +565,7 @@
             VMEM((count,) + piece, BF),
             VMEM((2, count) + piece, BF),
             VMEM((count,) + piece, F32),
-            VMEM(weights.shape, BF),
+            VMEM(halves, BF),
             VMEM((2, two_width, rows), F32),
             VMEM((2, two_width, rows), BF),
             sem((2, 2, steps, 3)),
@@ -482,71 +579,42 @@
             sem((2, count)),
             sem((2, count)),
             sem((4,)),
+            sem((2, 3)),
         ],
         compiler_params=pltpu.CompilerParams(
-            collective_id=1, has_side_effects=True, vmem_limit_bytes=62 << 20
+            collective_id=1, has_side_effects=True, vmem_limit_bytes=63 << 20
         ),
         name="layer",
-    )(ints, flts, sent, weights)
+    )(plan, before_it, last_of, ids, gates, both, w_gate, w_up, w_down)
 
 
 def body(tokens, cotangent, slot_ids, gates, plan, w_gate, w_up, w_down):
     count = lax.axis_size("expert")
     ring = lax.axis_size("dp")
     token_count, width = tokens.shape
-    choose = slot_ids.shape[1]
-    hidden = w_gate.shape[2]
-    slots = 2 * count
-    capacity = 5 * token_count * choose // (4 * slots)
-    pair = 2 * capacity
-    columns = count * pair
-    rows = count * capacity
-    half = hidden // 2
-
-    named = slot_ids[:, :, None] == jnp.arange(slots, dtype=jnp.int32)
-    names = jnp.sum(named.astype(F32), axis=1)
-    t_ids = jnp.arange(token_count, dtype=jnp.int32)
-    before = (t_ids[:, None] > t_ids[None, :]).astype(BF)
-    turns = jnp.dot(before, names.astype(BF), preferred_element_type=F32)
-    turn = jnp.sum(jnp.where(named, turns[:, None, :], 0.0), axis=2).astype(jnp.int32)
-    place = (slot_ids % count) * pair + (slot_ids // count) * capacity + turn
-    column_ids = jnp.arange(columns, dtype=jnp.int32)
-    hits = place[:, :, None] == column_ids
-    chosen = jnp.sum(hits.astype(F32), axis=1).astype(BF)
-    weight = jnp.sum(jnp.where(hits, gates[:, :, None], 0.0), axis=1)
-    gate_of = jnp.sum(weight, axis=0)
-
-    both = jnp.concatenate([tokens, cotangent], axis=1)
-    picked = lax.dot_general(chosen, both, (((0,), (0,)), ((), ())), preferred_element_type=F32)
-    scale = jnp.where(jnp.arange(2 * width)[None, :] < width, 1.0, gate_of[:, None])
-    sent = (picked * scale).astype(BF).reshape(count, pair, 2 * width)
-    down_t = jnp.swapaxes(w_down[0], 0, 1)
-    flat = -(-3 * width // (8 * 16)) * 8 * 16
-    filler = jnp.zeros((flat - 3 * width, hidden), BF)
-    whole = jnp.concatenate([w_gate[0], w_up[0], down_t, filler])
-    weights = jnp.stack([whole[:, h * half : (h + 1) * half] for h in range(2)])
+    capacity = 5 * token_count * slot_ids.shape[1] // (4 * 2 * count)
 
     s_ids = jnp.arange(count, dtype=jnp.int32)
-    sought = jnp.concatenate([plan, s_ids])
-    limit = jnp.concatenate([s_ids, jnp.full((count,), count, jnp.int32)])
-    match = (plan[None, :] == sought[:, None]) & (s_ids[None, :] < limit[:, None])
-    found = jnp.max(jnp.where(match, s_ids[None, :], -1), axis=1)
-    ints = jnp.concatenate([plan, jnp.maximum(found, 0)]).reshape(3, count)
-    flts = (found >= 0).astype(F32).reshape(2, count)
-
-    returned, grads = layer(sent, weights, ints, flts, capacity, ring)
-    returned = returned.reshape(columns, 2 * width)
-    high = weight.astype(BF)
-    low = (weight - high.astype(F32)).astype(BF)
-    output = (
-        jnp.dot(high, returned[:, :width], preferred_element_type=F32)
-        + jnp.dot(low, returned[:, :width], preferred_element_type=F32)
-    ).astype(BF)
-    token_grad = jnp.dot(chosen, returned[:, width:], preferred_element_type=F32).astype(BF)
-
+    alike = (plan[None, :] == plan[:, None]) & (s_ids[None, :] < s_ids[:, None])
+    before_it = jnp.max(jnp.where(alike, s_ids[None, :], -1), axis=1)
+    last_of = jnp.max(jnp.where(plan[None, :] == s_ids[:, None], s_ids[None, :], -1), axis=1)
+
+    results, grads = layer(
+        plan,
+        before_it,
+        last_of,
+        slot_ids,
+        gates,
+        jnp.concatenate([tokens, cotangent], axis=1),
+        w_gate[0],
+        w_up[0],
+        jnp.swapaxes(w_down[0], 0, 1),
+        capacity,
+        ring,
+    )
     return (
-        output,
-        token_grad,
+        results[:, :width],
+        results[:, width:],
         grads[:width][None],
         grads[width : 2 * width][None],
         jnp.swapaxes(grads[2 * width :], 0, 1)[None],

time: 300 us -> 297 us (0.990)
  Pallas kernels: 267 us -> 281 us
  other arithmetic: 16 us -> 2.22 us
  matrix products: 11.3 us -> 0 us
  local copies, waits for them, and re-layouts: 5.17 us -> 12.7 us
    pallas_call x1, Pallas kernels: 267 us -> 281 us  [layer(): pl.pallas_call(functools.partial(layer_kernel, count, ring, capacity), ou...]
    dot_general x5 -> x0, matrix products: 11.3 us -> none  [the longest x1 3.42 us: body(): jnp.dot(chosen, returned[:, width:], preferred_element_type=F32).astype(BF)]
    concatenate x3 -> x1, other arithmetic: 7.58 us -> 0.79 us  [body(): jnp.concatenate([tokens, cotangent], axis=1)]
    unnamed x7 -> x6, local copies, waits for them, and re-layouts: 0.8 us -> 6.36 us
    reduce_sum x3 -> x0, other arithmetic: 5.07 us -> none  [the longest x1 3.51 us: body(): weight = jnp.sum(jnp.where(hits, gates[:, :, None], 0.0), axis=1)]
where the time goes in v2:
time: 297 us; the launch traced here: 296 us
  Pallas kernels  281 us (95%)
  local copies, waits for them, and re-layouts  12.7 us (4%)
    pallas_call x1, Pallas kernels, layer(): pl.pallas_call(functools.partial(layer_kernel, count, ring, capacity), ou...  281 us
    unnamed x6, local copies, waits for them, and re-layouts  6.36 us

profile of v2, /device:TPU:1, one launch (start us, length us, event | category | flops | bytes accessed | tf_op | source)
XLA Modules:
  0.0 296.2 jit_solution(7003133606680451497)
XLA Ops:
  0.6 1.4 select_reduce_fusion
  2.1 1.4 copy.21.ids
  3.5 1.4 copy.22.gates
  4.9 1.0 copy.19
  5.9 1.0 copy.20
  6.9 0.8 pad_maximum_fusion.both
  7.7 280.6 %layer.1 = (bf16[128,896]{1,0:T(8,128)(2,1)}, f32[1344,1024]{1,0:T(8,128)}) custom-call(s32[32]{0:T(128)} %plan.1, s32[32]{0:T(128)} %get-tuple-element.20.before_it, s32[32]{0:T(128)} %get-tuple-element.19.last_of, s32[128,8]{1,0:T(8,128)} %copy.21.ids, f32[128,8]{1,0:T(8,128)} %copy.22.gates, bf16[128,896]{1,0:T(8,128)(2,1)} %pad_maximum_fusion.both, ...), custom_call_target="tpu_custom_call" | custom-call | tf_op jit(solution)/shard_map/layer/pallas_call | solution.py:538
  288.3 1.1 fusion.1
  289.4 0.8 copy.24
  290.2 0.8 copy.23
  290.9 5.3 %slice_bitcast_fusion = (f32[1,1024,448]{1,2,0:T(8,128)}, f32[1,448,1024]{2,1,0:T(8,128)}, f32[1,448,1024]{2,1,0:T(8,128)}) fusion(f32[1344,1024]{1,0:T(8,128)} %get-tuple-element.8), kind=kLoop, calls=%fused_computation | loop fusion | bytes 11010048 | tf_op jit(solution)/shard_map/broadcast_in_dim | solution.py:620

commit v3 on v2

--- a/solution.py
+++ b/solution.py
@@ -94,14 +94,24 @@
             device_id={"expert": peer}, device_id_type=MESH,
         )
 
-    def exchange(src, dst, turn):
+    split = -(-width // 128) * 128
+
+    def exchange(src, dst, turn, first=0, stop=2 * width):
+        lanes = pl.ds(first, stop - first)
+
         def copy(i):
             peer = peer_of(i)
             return to_peer(
-                src.at[peer], dst.at[me], ex_send.at[turn, i], ex_recv.at[turn, i], peer
-            )
-
-        own = pltpu.make_async_copy(src.at[me], dst.at[me], local.at[2 + turn])
+                src.at[peer, :, lanes],
+                dst.at[me, :, lanes],
+                ex_send.at[turn, i],
+                ex_recv.at[turn, i],
+                peer,
+            )
+
+        own = pltpu.make_async_copy(
+            src.at[me, :, lanes], dst.at[me, :, lanes], local.at[2 + turn]
+        )
         own.start()
         each(count, 1, lambda i: copy(i).start())
 
@@ -145,9 +155,10 @@
                 staged.at[self.p, me], self.result.at[part_of(me)], local.at[1]
             )
 
-        def begin(self):
-            self.own_out().start()
-            each(count, 1, lambda i: self.out_copy(i).start())
+        def begin(self, first=1, stop=count):
+            if first == 1:
+                self.own_out().start()
+            each(stop, first, lambda i: self.out_copy(i).start())
 
         def pass_on(self):
             self.own_out().wait()
@@ -184,20 +195,18 @@
             self.own_back().wait()
             each(count, 1, lambda i: self.back_copy(i).wait())
 
-    def multiply_parts(w, k, p):
-        def for_input(m, src):
-            def tile(b):
-                lane = pl.ds(pl.multiple_of(b * 128, 128), 128)
-                parts[p, m, lane] = matmul(
-                    w[pl.ds(m * width, width), lane], src[k], 0, 0
-                ).astype(BF)
-
-            each(half_hidden // 128, 0, tile)
-
-        for m in range(3):
-            for_input(m, zs_ref if m == 2 else xs_ref)
-
-    tile_rows = width // 4
+    lane_tile = half_hidden // 2
+
+    def multiply_part(w, k, p, m):
+        src = zs_ref if m == 2 else xs_ref
+
+        def tile(b):
+            lane = pl.ds(pl.multiple_of(b * lane_tile, lane_tile), lane_tile)
+            parts[p, m, lane] = matmul(w[pl.ds(m * width, width), lane], src[k], 0, 0).astype(BF)
+
+        each(2, 0, tile)
+
+    tile_rows = width // 2
 
     def multiply_grads(acts, k, dst):
         for m in range(3):
@@ -209,7 +218,7 @@
                     src[k, pl.ds(row, tile_rows)], acts[m], 1, 1
                 ).astype(BF)
 
-            each(4, 0, tile)
+            each(2, 0, tile)
 
     def home_grads(h):
         lane = pl.ds(h * half_hidden, half_hidden)
@@ -223,7 +232,7 @@
                     src[0, pl.ds(row, tile_rows)], home_acts[h, m], 1, 1
                 ) + summed[h, at].astype(F32)
 
-            each(4, 0, tile)
+            each(2, 0, tile)
 
     def multiply_rows(w, acts, store):
         def tile(b):
@@ -237,7 +246,7 @@
                 + matmul(w[up], acts[1], 1, 0),
             )
 
-        each(4, 0, tile)
+        each(2, 0, tile)
 
     def keep_rows(k):
         def store(row, value):
@@ -311,11 +320,13 @@
         lane = lax.broadcasted_iota(jnp.int32, plain.shape, 1)
         results[...] = jnp.where(lane < width, scaled, plain).astype(BF)
 
-    def sort_rows():
+    def sort_rows(ref, first_lane, skip):
         sources = 8
         for n in range(rows // 128):
             first = min(128 * n // capacity, count - sources)
-            block = got[pl.ds(first, sources)].reshape(sources * pair, 2 * width)
+            block = got[pl.ds(first, sources), :, pl.ds(first_lane, split)].reshape(
+                sources * pair, split
+            )
             shape = (sources * pair, 128)
             r = lax.broadcasted_iota(jnp.int32, shape, 0)
             lane = lax.broadcasted_iota(jnp.int32, shape, 1) + 128 * n
@@ -324,9 +335,7 @@
             for k in range(2):
                 hit = (goes_to == lane) & (lax.div(inside, capacity) == k)
                 tile = matmul(block, jnp.where(hit, 1.0, 0.0).astype(BF), 0, 0)
-                at = pl.ds(128 * n, 128)
-                xs_ref[k, :, at] = tile[:width].astype(BF)
-                zs_ref[k, :, at] = tile[width:].astype(BF)
+                ref[k, :, pl.ds(128 * n, 128)] = tile[skip : skip + width].astype(BF)
 
     def unsort_rows(k, first):
         sources, window = 4, 256
@@ -352,7 +361,7 @@
 
         each(blocks, 0, block)
 
-    def over_dp(p, acts, early, middle, late):
+    def over_dp(p, acts, prepare, early, middle, late):
         def rows_of(c, d=None):
             base = lax.rem(c + 2 * ring, ring) * chunk
             if d is None:
@@ -409,6 +418,7 @@
             in_flight[d].append(copy)
 
         for m in range(3):
+            prepare(m)
             for d in sides:
                 launch(sum_copy(0, m, d), d)
         early()
@@ -447,8 +457,8 @@
                 for d in sides:
                     spread_copy(t - 1, m, d).wait_recv()
                     launch(spread_copy(t, m, d), d)
-            if t == 1:
-                late()
+            if t in late:
+                late[t]()
         for m in (2, 0, 1):
             for d in sides:
                 spread_copy(steps - 1, m, d).wait_recv()
@@ -467,51 +477,69 @@
     ]
     for m in range(3):
         place_copy(0, m).wait()
-    moves[0].begin()
+    moves[0].begin(1, count // 2)
     send_rows()
-    exchange(sent, got, 0)()
-    moves[0].pass_on()
-    sort_rows()
-    multiply_parts(weights.at[0], 0, 0)
-    for m in range(3):
-        place_copy(1, m).wait()
-
-    def next_weights():
-        moves[0].finish()
-        moves[1].begin()
-
-    over_dp(0, home_acts.at[0], nothing, next_weights, nothing)
-    multiply_parts(copied.at[0], 1, 1)
-
-    def home_rows():
-        moves[1].pass_on()
-        multiply_rows(weights.at[0], home_acts.at[0], keep_rows(0))
-
-    over_dp(1, rep_acts.at[0], home_rows, nothing, nothing)
+    exchange(sent, got, 0, 0, split)()
+    others = exchange(sent, got, 1, split)
+
+    def first_inputs(m):
+        if m == 0:
+            sort_rows(xs_ref, 0, 0)
+        if m == 2:
+            others()
+            sort_rows(zs_ref, 2 * width - split, split - width)
+        multiply_part(weights.at[0], 0, 0, m)
+
+    def more_weights():
+        moves[0].begin(count // 2, count)
+        for m in range(3):
+            place_copy(1, m).wait()
+
+    over_dp(0, home_acts.at[0], first_inputs, more_weights, moves[0].pass_on, {})
+    moves[0].finish()
+    moves[1].begin()
+    over_dp(
+        1,
+        rep_acts.at[0],
+        lambda m: multiply_part(copied.at[0], 1, 1, m),
+        nothing,
+        moves[1].pass_on,
+        {1: lambda: multiply_rows(weights.at[0], home_acts.at[0], keep_rows(0))},
+    )
     moves[1].finish()
-    multiply_parts(copied.at[1], 1, 0)
 
     def first_grads():
         multiply_grads(rep_acts.at[0], 1, slot_grads.at[0])
         moves[2].begin()
-        multiply_rows(copied.at[0], rep_acts.at[0], keep_rows(1))
-
-    over_dp(0, rep_acts.at[1], first_grads, moves[2].pass_on, nothing)
-    multiply_parts(weights.at[1], 0, 1)
-    moves[2].finish()
+
+    over_dp(
+        0,
+        rep_acts.at[1],
+        lambda m: multiply_part(copied.at[1], 1, 0, m),
+        first_grads,
+        moves[2].pass_on,
+        {1: lambda: multiply_rows(copied.at[0], rep_acts.at[0], keep_rows(1))},
+    )
 
     def second_grads():
+        moves[2].finish()
         multiply_grads(rep_acts.at[1], 1, slot_grads.at[1])
         moves[3].begin()
 
-    def replica_rows():
-        multiply_rows(copied.at[1], rep_acts.at[1], end_rows(1))
-        unsort_rows(1, True)
-
-    over_dp(1, home_acts.at[1], second_grads, moves[3].pass_on, replica_rows)
+    over_dp(
+        1,
+        home_acts.at[1],
+        lambda m: multiply_part(weights.at[1], 0, 1, m),
+        second_grads,
+        moves[3].pass_on,
+        {
+            1: lambda: multiply_rows(copied.at[1], rep_acts.at[1], end_rows(1)),
+            2: lambda: unsort_rows(1, True),
+        },
+    )
     multiply_rows(weights.at[1], home_acts.at[1], end_rows(0))
     unsort_rows(0, False)
-    done = exchange(got, returned, 1)
+    done = exchange(got, returned, 2)
     home_grads(0)
     moves[3].finish()
     home_grads(1)
@@ -576,9 +604,9 @@
             sem((2, count)),
             sem((2, count)),
             sem((2, count)),
-            sem((2, count)),
-            sem((2, count)),
-            sem((4,)),
+            sem((3, count)),
+            sem((3, count)),
+            sem((5,)),
             sem((2, 3)),
         ],
         compiler_params=pltpu.CompilerParams(

time: 297 us -> 274 us (0.923)
  Pallas kernels: 281 us -> 258 us
    pallas_call x1, Pallas kernels: 281 us -> 258 us  [layer(): pl.pallas_call(functools.partial(layer_kernel, count, ring, capacity), ou...]
where the time goes in v3:
time: 274 us
  Pallas kernels  258 us (94%)
  local copies, waits for them, and re-layouts  12.7 us (5%)
    pallas_call x1, Pallas kernels, layer(): pl.pallas_call(functools.partial(layer_kernel, count, ring, capacity), ou...  258 us
    unnamed x6, local copies, waits for them, and re-layouts  6.36 us

profile of v3, /device:TPU:1, one launch (start us, length us, event | category | flops | bytes accessed | tf_op | source)
XLA Modules:
  0.0 273.8 jit_solution(17837192713535076514)
XLA Ops:
  0.6 1.4 select_reduce_fusion
  2.1 1.4 copy.21.ids
  3.5 1.4 copy.22.gates
  4.9 1.0 copy.19
  5.9 1.0 copy.20
  6.9 0.8 pad_maximum_fusion.both
  7.7 258.2 %layer.1 = (bf16[128,896]{1,0:T(8,128)(2,1)}, f32[1344,1024]{1,0:T(8,128)}) custom-call(s32[32]{0:T(128)} %plan.1, s32[32]{0:T(128)} %get-tuple-element.20.before_it, s32[32]{0:T(128)} %get-tuple-element.19.last_of, s32[128,8]{1,0:T(8,128)} %copy.21.ids, f32[128,8]{1,0:T(8,128)} %copy.22.gates, bf16[128,896]{1,0:T(8,128)(2,1)} %pad_maximum_fusion.both, ...), custom_call_target="tpu_custom_call" | custom-call | tf_op jit(solution)/shard_map/layer/pallas_call | solution.py:566
  265.9 1.1 fusion.1
  267.0 0.8 copy.24
  267.8 0.8 copy.23
  268.6 5.3 %slice_bitcast_fusion = (f32[1,1024,448]{1,2,0:T(8,128)}, f32[1,448,1024]{2,1,0:T(8,128)}, f32[1,448,1024]{2,1,0:T(8,128)}) fusion(f32[1344,1024]{1,0:T(8,128)} %get-tuple-element.8), kind=kLoop, calls=%fused_computation | loop fusion | bytes 11010048 | tf_op jit(solution)/shard_map/broadcast_in_dim | solution.py:648

commit v4 on v3

--- a/solution.py
+++ b/solution.py
@@ -46,8 +46,8 @@
 
 
 def layer_kernel(
-    count, ring, capacity, plan, before_it, last_of, ids, gates, both, w_gate, w_up, w_down,
-    results, grads,
+    count, ring, capacity, plan, before_it, last_of, ids_t, gates_t, tokens_t, cotangent_t, w_gate, w_up, w_down,
+    output_t, token_grad_t, grads,
     weights, sent, returned, chosen, high, low, got, home_acts, summed, xs_ref, zs_ref, copied, parts, rep_acts, landed, held_even, held_odd, staged, run, slot_grads, rows_acc, made,
     z_send, z_recv, g_send, g_recv, out_send, out_recv, back_send, back_recv, ex_send, ex_recv, local, placed,
 ):
@@ -266,7 +266,10 @@
     tile_sources = count // row_tiles
 
     def send_rows():
-        tokens, choose = ids.shape
+        choose, tokens = ids_t.shape
+        ids = jnp.transpose(ids_t[...])
+        gates = jnp.transpose(gates_t[...])
+        both = jnp.transpose(jnp.concatenate([tokens_t[...], cotangent_t[...]], axis=0))
         slot = lax.broadcasted_iota(jnp.int32, (tokens, 2 * count), 1)
         named = [ids[:, k : k + 1] == slot for k in range(choose)]
         names = sum(jnp.where(hit, 1.0, 0.0) for hit in named)
@@ -297,8 +300,8 @@
             top = weight.astype(BF)
             high[:, at] = top
             low[:, at] = (weight - top.astype(F32)).astype(BF)
-            plain = matmul(chosen[:, at], both[...], 0, 0)
-            scaled = matmul(high[:, at], both[...], 0, 0) + matmul(low[:, at], both[...], 0, 0)
+            plain = matmul(chosen[:, at], both, 0, 0)
+            scaled = matmul(high[:, at], both, 0, 0) + matmul(low[:, at], both, 0, 0)
             lane = lax.broadcasted_iota(jnp.int32, plain.shape, 1)
             sent[pl.ds(n * tile_sources, tile_sources)] = (
                 jnp.where(lane < width, plain, scaled)
@@ -317,8 +320,8 @@
             scaled = scaled + (
                 matmul(high[:, at], block, 1, 0) + matmul(low[:, at], block, 1, 0)
             )
-        lane = lax.broadcasted_iota(jnp.int32, plain.shape, 1)
-        results[...] = jnp.where(lane < width, scaled, plain).astype(BF)
+        output_t[...] = jnp.transpose(scaled)[:width].astype(BF)
+        token_grad_t[...] = jnp.transpose(plain)[width:].astype(BF)
 
     def sort_rows(ref, first_lane, skip):
         sources = 8
@@ -547,10 +550,13 @@
     add_rows()
 
 
-def layer(plan, before_it, last_of, ids, gates, both, w_gate, w_up, w_down, capacity, ring):
+def layer(
+    plan, before_it, last_of, ids_t, gates_t, tokens_t, cotangent_t, w_gate, w_up, w_down, capacity, ring
+):
     count = plan.shape[0]
-    tokens, two_width = both.shape
+    tokens = ids_t.shape[1]
     width, hidden = w_gate.shape
+    two_width = 2 * width
     half_hidden = hidden // 2
     pair = 2 * capacity
     rows = count * capacity
@@ -566,13 +572,14 @@
     return pl.pallas_call(
         functools.partial(layer_kernel, count, ring, capacity),
         out_shape=(
-            jax.ShapeDtypeStruct((tokens, two_width), BF),
+            jax.ShapeDtypeStruct((width, tokens), BF),
+            jax.ShapeDtypeStruct((width, tokens), BF),
             jax.ShapeDtypeStruct((3 * width, hidden), F32),
         ),
         in_specs=[pl.BlockSpec(memory_space=pltpu.SMEM)] * 3
-        + [pl.BlockSpec(memory_space=VMEM)] * 3
+        + [pl.BlockSpec(memory_space=VMEM)] * 4
         + [pl.BlockSpec(memory_space=pl.ANY)] * 3,
-        out_specs=[pl.BlockSpec(memory_space=VMEM)] * 2,
+        out_specs=[pl.BlockSpec(memory_space=VMEM)] * 3,
         scratch_shapes=[
             VMEM(halves, BF),
             VMEM(blocks, BF),
@@ -613,7 +620,7 @@
             collective_id=1, has_side_effects=True, vmem_limit_bytes=63 << 20
         ),
         name="layer",
-    )(plan, before_it, last_of, ids, gates, both, w_gate, w_up, w_down)
+    )(plan, before_it, last_of, ids_t, gates_t, tokens_t, cotangent_t, w_gate, w_up, w_down)
 
 
 def body(tokens, cotangent, slot_ids, gates, plan, w_gate, w_up, w_down):
@@ -627,13 +634,14 @@
     before_it = jnp.max(jnp.where(alike, s_ids[None, :], -1), axis=1)
     last_of = jnp.max(jnp.where(plan[None, :] == s_ids[:, None], s_ids[None, :], -1), axis=1)
 
-    results, grads = layer(
+    output_t, token_grad_t, grads = layer(
         plan,
         before_it,
         last_of,
-        slot_ids,
-        gates,
-        jnp.concatenate([tokens, cotangent], axis=1),
+        slot_ids.T,
+        gates.T,
+        tokens.T,
+        cotangent.T,
         w_gate[0],
         w_up[0],
         jnp.swapaxes(w_down[0], 0, 1),
@@ -641,8 +649,8 @@
         ring,
     )
     return (
-        results[:, :width],
-        results[:, width:],
+        output_t.T,
+        token_grad_t.T,
         grads[:width][None],
         grads[width : 2 * width][None],
         jnp.swapaxes(grads[2 * width :], 0, 1)[None],

time: 274 us -> 267 us (0.974)
  local copies, waits for them, and re-layouts: 12.7 us -> 6.59 us
    unnamed x6, local copies, waits for them, and re-layouts: 6.36 us -> 1.3 us
where the time goes in v4:
time: 267 us
  Pallas kernels  259 us (97%)
  local copies, waits for them, and re-layouts  6.59 us (2%)
    pallas_call x1, Pallas kernels, layer(): pl.pallas_call(functools.partial(layer_kernel, count, ring, capacity), ou...  259 us

profile of v4, /device:TPU:1, one launch (start us, length us, event | category | flops | bytes accessed | tf_op | source)
XLA Modules:
  0.0 267.3 jit_solution(10985431070576491213)
XLA Ops:
  0.6 1.4 select_reduce_fusion
  2.1 258.6 %layer.1 = (bf16[448,128]{1,0:T(8,128)(2,1)}, bf16[448,128]{1,0:T(8,128)(2,1)}, f32[1344,1024]{1,0:T(8,128)}) custom-call(s32[32]{0:T(128)} %plan.1, s32[32]{0:T(128)} %get-tuple-element.12.before_it, s32[32]{0:T(128)} %get-tuple-element.11.last_of, s32[8,128]{1,0:T(8,128)} %bitcast.26, f32[8,128]{1,0:T(8,128)} %bitcast.27, bf16[448,128]{1,0:T(8,128)(2,1)} %bitcast.24, ...), custom_call_target="tpu_custom_call" | custom-call | tf_op jit(solution)/shard_map/layer/pallas_call | solution.py:572
  260.7 0.0 copy-start.1
  260.7 0.0 copy-start
  260.7 5.3 %slice_bitcast_fusion = (f32[1,1024,448]{1,2,0:T(8,128)}, f32[1,448,1024]{2,1,0:T(8,128)}, f32[1,448,1024]{2,1,0:T(8,128)}) fusion(f32[1344,1024]{1,0:T(8,128)} %get-tuple-element.10), kind=kLoop, calls=%fused_computation | loop fusion | bytes 11010048 | tf_op jit(solution)/shard_map/broadcast_in_dim | solution.py:656
  266.0 0.0 copy-done.1
  266.0 0.6 copy.15
  266.6 0.0 copy-done
  266.7 0.6 copy.16
Async XLA Ops:
  260.7 5.3 %copy-start.1 = (bf16[448,128]{1,0:T(8,128)(2,1)S(1)}, bf16[448,128]{1,0:T(8,128)(2,1)}, u32[]{:S(2)}) copy-start(bf16[448,128]{1,0:T(8,128)(2,1)} %get-tuple-element.8) | copy-start | bytes 344068
  260.7 6.0 %copy-start = (bf16[448,128]{1,0:T(8,128)(2,1)S(1)}, bf16[448,128]{1,0:T(8,128)(2,1)}, u32[]{:S(2)}) copy-start(bf16[448,128]{1,0:T(8,128)(2,1)} %get-tuple-element.9) | copy-start | bytes 344068
